TPU v7x, 768 devices: a whole 4x8x12 slice. The times are simulated.
768 devices in a mesh: lon: 32 (over z_hi, y), lat: 24 (over x, z_lo, core).
Axes of the slice: x: 4, y: 8, z: 12 (z_hi: 4, z_lo: 3; z = z_hi * 3 + z_lo), core: 2. Of those that a mesh axis runs over, the one named last changes fastest.
Arguments:
- fields: bfloat16 [384, 1024, 128], P('lat', 'lon'), may hold values from -6 to 6
- cotangent: bfloat16 [384, 1024, 128], P('lat', 'lon'), may hold values from -6 to 6
- weight_first: bfloat16 [3, 3, 128, 128], replicated, may hold values from -0.1875 to 0.1875
- weight_second: bfloat16 [3, 3, 128, 128], replicated, may hold values from -0.1875 to 0.1875
Outputs:
- output: bfloat16 [384, 1024, 128], P('lat', 'lon')
- back_fields: bfloat16 [384, 1024, 128], P('lat', 'lon')
- grad_first: float32 [3, 3, 128, 128], replicated
- grad_second: float32 [3, 3, 128, 128], replicated
All inputs are finite; a program needn't handle non-finite values.
Results may differ from a plain program's by a relative error of at most 0.0034.
Values may be sent and summed in bfloat16 or wider, within the bound.
No kernel may reach another device: no remote copies, remote signals or barrier semaphores. Data moves between devices by JAX's collectives and lax.ppermute only.
A program may use at most 32 MiB of HBM per device.

v0:
```python
import math

import jax
import jax.numpy as jnp
from jax import lax
from jax.sharding import PartitionSpec as P


def shifted(x, axis, by):
    devices = lax.axis_size(axis)
    return lax.ppermute(x, axis, [(i, (i + by) % devices) for i in range(devices)])


def extended_2(x, sides, width, wrap):
    for axis, dim in sides:
        devices, length = (lax.axis_size(axis), x.shape[dim])
        up = [(i, (i + 1) % devices) for i in range(devices if wrap else devices - 1)]
        down = [(j, i) for i, j in up]
        last = lax.slice_in_dim(x, length - width, length, axis=dim)
        initial = lax.slice_in_dim(x, 0, width, axis=dim)
        before = lax.ppermute(last, axis, up)
        after = lax.ppermute(initial, axis, down)
        x = jnp.concatenate([before, x, after], axis=dim)
    return x


def extend_stack(stacked, north_pole, south_pole):
    row_count = stacked.shape[1]
    half_way = lax.axis_size("lon") // 2
    border = jnp.concatenate([stacked[:, 0:1], stacked[:, row_count - 1 : row_count]], axis=1)
    remote = shifted(border, "lon", half_way)
    with_rows = extended_2(stacked, (("lat", 1),), 1, False)
    top_row = jnp.where(north_pole, remote[:, 0:1], with_rows[:, 0:1])
    bottom_row = jnp.where(south_pole, remote[:, 1:2], with_rows[:, row_count + 1 : row_count + 2])
    with_rows = jnp.concatenate([top_row, with_rows[:, 1 : row_count + 1], bottom_row], axis=1)
    result = extended_2(with_rows, (("lon", 2),), 1, True)
    return result


def tap_patches(padded, row_count, col_count):
    return jnp.concatenate(
        [
            padded[tap_row : tap_row + row_count, tap_col : tap_col + col_count]
            for tap_row in range(3)
            for tap_col in range(3)
        ],
        axis=-1,
    )


def apply_kernel(patches, weight):
    channels = weight.shape[-1]
    return jnp.einsum(
        "rlk,kd->rld",
        patches,
        weight.reshape(9 * channels, channels),
        preferred_element_type=jnp.float32,
    )


def outer_sums(patches, upstream):
    channels = upstream.shape[-1]
    summed = jnp.einsum("rlk,rld->kd", patches, upstream, preferred_element_type=jnp.float32)
    return summed.reshape(3, 3, channels, channels)


def pole_term(pole_row, kernel_row, col_count):
    channels = kernel_row.shape[-1]
    pieces = jnp.concatenate(
        [pole_row[:, tap_col : tap_col + col_count] for tap_col in range(3)], axis=-1
    )
    flipped = jnp.transpose(kernel_row[::-1], (0, 2, 1)).reshape(3 * channels, channels)
    return jnp.einsum("rlk,kd->rld", pieces, flipped, preferred_element_type=jnp.float32)


def adjoint_conv(padded, weight, north_pole, south_pole):
    row_count = padded.shape[0] - 2
    col_count = padded.shape[1] - 2
    zero_row = jnp.zeros_like(padded[0:1])
    top_row = jnp.where(north_pole, zero_row, padded[0:1])
    bottom_row = jnp.where(south_pole, zero_row, padded[row_count + 1 : row_count + 2])
    masked = jnp.concatenate([top_row, padded[1 : row_count + 1], bottom_row], axis=0)
    flipped = jnp.transpose(weight[::-1, ::-1], (0, 1, 3, 2))
    summed = apply_kernel(tap_patches(masked, row_count, col_count), flipped)
    north_term = pole_term(padded[0:1], weight[0], col_count)
    south_term = pole_term(padded[row_count + 1 : row_count + 2], weight[2], col_count)
    summed = summed.at[0:1].add(jnp.where(north_pole, north_term, 0.0))
    summed = summed.at[row_count - 1 : row_count].add(jnp.where(south_pole, south_term, 0.0))
    return summed


def per_device(fields, cotangent, weight_first, weight_second):
    row_count, col_count, channels = fields.shape
    lat_place = lax.axis_index("lat")
    north_pole = lat_place == 0
    south_pole = lat_place == lax.axis_size("lat") - 1
    extended = extend_stack(jnp.stack([fields, cotangent]), north_pole, south_pole)
    patches_fields = tap_patches(extended[0], row_count, col_count)
    first_sum = apply_kernel(patches_fields, weight_first)
    hidden = jax.nn.silu(first_sum).astype(jnp.bfloat16)
    padded_hidden = extend_stack(hidden[None], north_pole, south_pole)[0]
    back_hidden = adjoint_conv(extended[1], weight_second, north_pole, south_pole)
    sigmoid_first = jax.nn.sigmoid(first_sum)
    back_first = (back_hidden * sigmoid_first * (1.0 + first_sum * (1.0 - sigmoid_first))).astype(
        jnp.bfloat16
    )
    padded_back = extend_stack(back_first[None], north_pole, south_pole)[0]
    patches_hidden = tap_patches(padded_hidden, row_count, col_count)
    second_sum = apply_kernel(patches_hidden, weight_second)
    output = (fields.astype(jnp.float32) + second_sum).astype(jnp.bfloat16)
    cells_total = row_count * lax.axis_size("lat") * col_count * lax.axis_size("lon")
    grad_scale = 1.0 / math.sqrt(cells_total)
    grad_second = outer_sums(patches_hidden, cotangent) * grad_scale
    grad_first = outer_sums(patches_fields, back_first) * grad_scale
    back_fields = (
        cotangent.astype(jnp.float32)
        + adjoint_conv(padded_back, weight_first, north_pole, south_pole)
    ).astype(jnp.bfloat16)
    grad_first, grad_second = lax.psum((grad_first, grad_second), ("lon", "lat"))
    return (output, back_fields, grad_first, grad_second)


def solution(mesh):
    return jax.shard_map(
        per_device,
        mesh=mesh,
        in_specs=(P("lat", "lon", None), P("lat", "lon", None), P(), P()),
        out_specs=(P("lat", "lon", None), P("lat", "lon", None), P(), P()),
        check_vma=False,
    )
```

profile of v0, /device:TPU:1, one launch (start us, length us, event | category | flops | bytes accessed | tf_op | source)
XLA Modules:
  0.0 599.1 jit_solution(6035221340033208116)
XLA Ops:
  7.2 0.8 pad_maximum_fusion.11
  8.1 5.4 collective-permute-start.1
  13.4 8.3 %collective-permute-start.2 = (bf16[2,1,32,128]{3,2,1,0:T(8,128)(2,1)S(1)}, bf16[2,1,32,128]{3,2,1,0:T(8,128)(2,1)S(1)}, u32[]{:S(2)}, u32[]{:S(2)}) collective-permute-start(bf16[2,1,32,128]{3,2,1,0:T(8,128)(2,1)S(1)} %get-tuple-element.73), channel_id=1, source_target_pairs={{1,0},{2,1},{3,2},{4,3},{5,4},{6,5},{7,6},{8,7},{9,8},{10,9},{11,1... | collective-permute-start | bytes 49160 | tf_op jit(solution)/shard_map/ppermute | solution.py:22
  21.8 8.2 %collective-permute-start = (bf16[2,2,32,128]{3,2,1,0:T(8,128)(2,1)S(1)}, bf16[2,2,32,128]{3,2,1,0:T(8,128)(2,1)S(1)}, u32[]{:S(2)}, u32[]{:S(2)}) collective-permute-start(bf16[2,2,32,128]{3,2,1,0:T(8,128)(2,1)S(1)} %pad_maximum_fusion.6), channel_id=1, source_target_pairs={{0,384},{24,408},{48,432},{72,456},{96,480},{120,504},{144,528},{1... | collective-permute-start | bytes 98312 | tf_op jit(solution)/shard_map/ppermute | solution.py:11
  30.0 1.2 copy.11
  31.2 0.2 copy.8
  31.4 1.6 collective-permute-done
  33.1 1.9 collective-permute-start.3
  35.1 9.6 %collective-permute-start.4 = (bf16[2,18,1,128]{3,2,1,0:T(2,128)(2,1)S(1)}, bf16[2,18,1,128]{3,2,1,0:T(2,128)(2,1)S(1)}, u32[]{:S(2)}, u32[]{:S(2)}) collective-permute-start(bf16[2,18,1,128]{3,2,1,0:T(2,128)(2,1)S(1)} %get-tuple-element.69), channel_id=1, source_target_pairs={{24,0},{48,24},{72,48},{96,72},{120,96},{144,120},{168,144},{192,1... | collective-permute-start | bytes 27656 | tf_op jit(solution)/shard_map/ppermute | solution.py:22
  44.8 0.7 collective-permute-done.4
  45.5 0.2 pad_maximum_fusion
  46.8 0.5 fusion.62
  47.7 0.5 multiply_convert_fusion
  48.3 5.8 collective-permute-start.6
  54.1 1.9 collective-permute-start.7
  56.1 3.6 collective-permute-start.11
  59.7 1.9 collective-permute-start.12
  61.7 5.7 collective-permute-start.5
  67.3 5.9 collective-permute-start.10
  73.3 1.3 fusion.1
  74.6 3.5 collective-permute-done.10
  78.2 1.9 collective-permute-start.13
  80.1 9.7 %collective-permute-start.14 = (bf16[1,18,1,128]{3,2,1,0:T(2,128)(2,1)S(1)}, bf16[1,18,1,128]{3,2,1,0:T(2,128)(2,1)S(1)}, u32[]{:S(2)}, u32[]{:S(2)}) collective-permute-start(bf16[1,18,1,128]{3,2,1,0:T(2,128)(2,1)S(1)} %get-tuple-element.77), channel_id=1, source_target_pairs={{24,0},{48,24},{72,48},{96,72},{120,96},{144,120},{168,144},{192,1... | collective-permute-start | bytes 13832 | tf_op jit(solution)/shard_map/ppermute | solution.py:22
  89.8 1.9 collective-permute-start.8
  91.7 8.5 %collective-permute-start.9 = (bf16[1,18,1,128]{3,2,1,0:T(2,128)(2,1)S(1)}, bf16[1,18,1,128]{3,2,1,0:T(2,128)(2,1)S(1)}, u32[]{:S(2)}, u32[]{:S(2)}) collective-permute-start(bf16[1,18,1,128]{3,2,1,0:T(2,128)(2,1)S(1)} %get-tuple-element.79), channel_id=1, source_target_pairs={{24,0},{48,24},{72,48},{96,72},{120,96},{144,120},{168,144},{192,1... | collective-permute-start | bytes 13832 | tf_op jit(solution)/shard_map/ppermute | solution.py:22
  101.6 1.3 fusion
  102.9 0.5 fusion.63
  103.7 0.7 add_convert_fusion
  104.4 1.1 fusion.2
  105.5 483.9 %all-reduce.3.cloned.1.call-done = (f32[3,3,128,128]{3,2,1,0:T(8,128)}, f32[3,3,128,128]{3,2,1,0:T(8,128)}) async-done(((f32[3,3,128,128]{3,2,1,0:T(8,128)}, f32[3,3,128,128]{3,2,1,0:T(8,128)}), (f32[3,3,128,128]{3,2,1,0:T(8,128)}, f32[3,3,128,128]{3,2,1,0:T(8,128)})) %all-reduce.3.cloned.1.call-update) | async-done | bytes 1179664 | tf_op jit(solution)/shard_map/psum | solution.py:119
  589.4 2.0 copy.52
  591.4 0.8 copy.53
  (93 shorter events, 3.2 us)
Async XLA Ops:
  7.2 25.9 %copy-start = (bf16[16,32,128]{2,1,0:T(8,128)(2,1)S(1)}, bf16[16,32,128]{2,1,0:T(8,128)(2,1)}, u32[]{:S(2)}) copy-start(bf16[16,32,128]{2,1,0:T(8,128)(2,1)} %param.13) | copy-start | bytes 393220
  7.2 25.9 %copy-start.1 = (bf16[16,32,128]{2,1,0:T(8,128)(2,1)S(1)}, bf16[16,32,128]{2,1,0:T(8,128)(2,1)}, u32[]{:S(2)}) copy-start(bf16[16,32,128]{2,1,0:T(8,128)(2,1)} %param.12) | copy-start | bytes 393220
  7.2 24.0 %copy-start.2 = (bf16[3,3,128,128]{3,2,1,0:T(8,128)(2,1)S(1)}, bf16[3,3,128,128]{3,2,1,0:T(8,128)(2,1)}, u32[]{:S(2)}) copy-start(bf16[3,3,128,128]{3,2,1,0:T(8,128)(2,1)} %param.15) | copy-start | bytes 884740
  7.2 582.2 %all-reduce.3.cloned.1.call-start = ((), (), s32[]{:S(2)}) async-start(), calls=%async_computation | async-start | bytes 2359296 | tf_op jit(solution)/shard_map/psum | solution.py:119
  8.1 23.3 %collective-permute-start.1 = (bf16[2,1,32,128]{3,2,1,0:T(8,128)(2,1)S(1)}, bf16[2,1,32,128]{3,2,1,0:T(8,128)(2,1)S(1)}, u32[]{:S(2)}, u32[]{:S(2)}) collective-permute-start(bf16[2,1,32,128]{3,2,1,0:T(8,128)(2,1)S(1)} %get-tuple-element.72), channel_id=1, source_target_pairs={{0,1},{1,2},{2,3},{3,4},{4,5},{5,6},{6,7},{7,8},{8,9},{9,10},{10,1... | collective-permute-start | bytes 49160 | tf_op jit(solution)/shard_map/ppermute | solution.py:21
  13.4 18.0 %collective-permute-start.2 = (bf16[2,1,32,128]{3,2,1,0:T(8,128)(2,1)S(1)}, bf16[2,1,32,128]{3,2,1,0:T(8,128)(2,1)S(1)}, u32[]{:S(2)}, u32[]{:S(2)}) collective-permute-start(bf16[2,1,32,128]{3,2,1,0:T(8,128)(2,1)S(1)} %get-tuple-element.73), channel_id=1, source_target_pairs={{1,0},{2,1},{3,2},{4,3},{5,4},{6,5},{7,6},{8,7},{9,8},{10,9},{11,1... | collective-permute-start | bytes 49160 | tf_op jit(solution)/shard_map/ppermute | solution.py:22
  21.8 11.3 %collective-permute-start = (bf16[2,2,32,128]{3,2,1,0:T(8,128)(2,1)S(1)}, bf16[2,2,32,128]{3,2,1,0:T(8,128)(2,1)S(1)}, u32[]{:S(2)}, u32[]{:S(2)}) collective-permute-start(bf16[2,2,32,128]{3,2,1,0:T(8,128)(2,1)S(1)} %pad_maximum_fusion.6), channel_id=1, source_target_pairs={{0,384},{24,408},{48,432},{72,456},{96,480},{120,504},{144,528},{1... | collective-permute-start | bytes 98312 | tf_op jit(solution)/shard_map/ppermute | solution.py:11
  33.1 11.7 %collective-permute-start.3 = (bf16[2,18,1,128]{3,2,1,0:T(2,128)(2,1)S(1)}, bf16[2,18,1,128]{3,2,1,0:T(2,128)(2,1)S(1)}, u32[]{:S(2)}, u32[]{:S(2)}) collective-permute-start(bf16[2,18,1,128]{3,2,1,0:T(2,128)(2,1)S(1)} %get-tuple-element.68), channel_id=1, source_target_pairs={{0,24},{24,48},{48,72},{72,96},{96,120},{120,144},{144,168},{168,1... | collective-permute-start | bytes 27656 | tf_op jit(solution)/shard_map/ppermute | solution.py:21
  35.1 10.5 %collective-permute-start.4 = (bf16[2,18,1,128]{3,2,1,0:T(2,128)(2,1)S(1)}, bf16[2,18,1,128]{3,2,1,0:T(2,128)(2,1)S(1)}, u32[]{:S(2)}, u32[]{:S(2)}) collective-permute-start(bf16[2,18,1,128]{3,2,1,0:T(2,128)(2,1)S(1)} %get-tuple-element.69), channel_id=1, source_target_pairs={{24,0},{48,24},{72,48},{96,72},{120,96},{144,120},{168,144},{192,1... | collective-permute-start | bytes 27656 | tf_op jit(solution)/shard_map/ppermute | solution.py:22
  46.8 1.0 copy-start.4
  48.3 19.0 %collective-permute-start.6 = (bf16[1,1,32,128]{3,2,1,0:T(8,128)(2,1)S(1)}, bf16[1,1,32,128]{3,2,1,0:T(8,128)(2,1)S(1)}, u32[]{:S(2)}, u32[]{:S(2)}) collective-permute-start(bf16[1,1,32,128]{3,2,1,0:T(8,128)(2,1)S(1)} %get-tuple-element.82), channel_id=1, source_target_pairs={{0,1},{1,2},{2,3},{3,4},{4,5},{5,6},{6,7},{7,8},{8,9},{9,10},{10,1... | collective-permute-start | bytes 24584 | tf_op jit(solution)/shard_map/ppermute | solution.py:21
  54.1 20.5 %collective-permute-start.7 = (bf16[1,1,32,128]{3,2,1,0:T(8,128)(2,1)S(1)}, bf16[1,1,32,128]{3,2,1,0:T(8,128)(2,1)S(1)}, u32[]{:S(2)}, u32[]{:S(2)}) collective-permute-start(bf16[1,1,32,128]{3,2,1,0:T(8,128)(2,1)S(1)} %get-tuple-element.83), channel_id=1, source_target_pairs={{1,0},{2,1},{3,2},{4,3},{5,4},{6,5},{7,6},{8,7},{9,8},{10,9},{11,1... | collective-permute-start | bytes 24584 | tf_op jit(solution)/shard_map/ppermute | solution.py:22
  56.1 18.5 %collective-permute-start.11 = (bf16[1,1,32,128]{3,2,1,0:T(8,128)(2,1)S(1)}, bf16[1,1,32,128]{3,2,1,0:T(8,128)(2,1)S(1)}, u32[]{:S(2)}, u32[]{:S(2)}) collective-permute-start(bf16[1,1,32,128]{3,2,1,0:T(8,128)(2,1)S(1)} %get-tuple-element.80), channel_id=1, source_target_pairs={{0,1},{1,2},{2,3},{3,4},{4,5},{5,6},{6,7},{7,8},{8,9},{9,10},{10,1... | collective-permute-start | bytes 24584 | tf_op jit(solution)/shard_map/ppermute | solution.py:21
  59.7 14.9 %collective-permute-start.12 = (bf16[1,1,32,128]{3,2,1,0:T(8,128)(2,1)S(1)}, bf16[1,1,32,128]{3,2,1,0:T(8,128)(2,1)S(1)}, u32[]{:S(2)}, u32[]{:S(2)}) collective-permute-start(bf16[1,1,32,128]{3,2,1,0:T(8,128)(2,1)S(1)} %get-tuple-element.81), channel_id=1, source_target_pairs={{1,0},{2,1},{3,2},{4,3},{5,4},{6,5},{7,6},{8,7},{9,8},{10,9},{11,1... | collective-permute-start | bytes 24584 | tf_op jit(solution)/shard_map/ppermute | solution.py:22
  61.7 13.0 %collective-permute-start.5 = (bf16[1,2,32,128]{3,2,1,0:T(8,128)(2,1)S(1)}, bf16[1,2,32,128]{3,2,1,0:T(8,128)(2,1)S(1)}, u32[]{:S(2)}, u32[]{:S(2)}) collective-permute-start(bf16[1,2,32,128]{3,2,1,0:T(8,128)(2,1)S(1)} %pad_maximum_fusion.13), channel_id=1, source_target_pairs={{0,384},{24,408},{48,432},{72,456},{96,480},{120,504},{144,528},{1... | collective-permute-start | bytes 49160 | tf_op jit(solution)/shard_map/ppermute | solution.py:11
  67.3 10.8 %collective-permute-start.10 = (bf16[1,2,32,128]{3,2,1,0:T(8,128)(2,1)S(1)}, bf16[1,2,32,128]{3,2,1,0:T(8,128)(2,1)S(1)}, u32[]{:S(2)}, u32[]{:S(2)}) collective-permute-start(bf16[1,2,32,128]{3,2,1,0:T(8,128)(2,1)S(1)} %pad_maximum_fusion.14), channel_id=1, source_target_pairs={{0,384},{24,408},{48,432},{72,456},{96,480},{120,504},{144,528},{1... | collective-permute-start | bytes 49160 | tf_op jit(solution)/shard_map/ppermute | solution.py:11
  78.2 22.0 %collective-permute-start.13 = (bf16[1,18,1,128]{3,2,1,0:T(2,128)(2,1)S(1)}, bf16[1,18,1,128]{3,2,1,0:T(2,128)(2,1)S(1)}, u32[]{:S(2)}, u32[]{:S(2)}) collective-permute-start(bf16[1,18,1,128]{3,2,1,0:T(2,128)(2,1)S(1)} %get-tuple-element.76), channel_id=1, source_target_pairs={{0,24},{24,48},{48,72},{72,96},{96,120},{120,144},{144,168},{168,1... | collective-permute-start | bytes 13832 | tf_op jit(solution)/shard_map/ppermute | solution.py:21
  80.1 20.1 %collective-permute-start.14 = (bf16[1,18,1,128]{3,2,1,0:T(2,128)(2,1)S(1)}, bf16[1,18,1,128]{3,2,1,0:T(2,128)(2,1)S(1)}, u32[]{:S(2)}, u32[]{:S(2)}) collective-permute-start(bf16[1,18,1,128]{3,2,1,0:T(2,128)(2,1)S(1)} %get-tuple-element.77), channel_id=1, source_target_pairs={{24,0},{48,24},{72,48},{96,72},{120,96},{144,120},{168,144},{192,1... | collective-permute-start | bytes 13832 | tf_op jit(solution)/shard_map/ppermute | solution.py:22
  89.8 11.1 %collective-permute-start.8 = (bf16[1,18,1,128]{3,2,1,0:T(2,128)(2,1)S(1)}, bf16[1,18,1,128]{3,2,1,0:T(2,128)(2,1)S(1)}, u32[]{:S(2)}, u32[]{:S(2)}) collective-permute-start(bf16[1,18,1,128]{3,2,1,0:T(2,128)(2,1)S(1)} %get-tuple-element.78), channel_id=1, source_target_pairs={{0,24},{24,48},{48,72},{72,96},{96,120},{120,144},{144,168},{168,1... | collective-permute-start | bytes 13832 | tf_op jit(solution)/shard_map/ppermute | solution.py:21
  91.7 9.3 %collective-permute-start.9 = (bf16[1,18,1,128]{3,2,1,0:T(2,128)(2,1)S(1)}, bf16[1,18,1,128]{3,2,1,0:T(2,128)(2,1)S(1)}, u32[]{:S(2)}, u32[]{:S(2)}) collective-permute-start(bf16[1,18,1,128]{3,2,1,0:T(2,128)(2,1)S(1)} %get-tuple-element.79), channel_id=1, source_target_pairs={{24,0},{48,24},{72,48},{96,72},{120,96},{144,120},{168,144},{192,1... | collective-permute-start | bytes 13832 | tf_op jit(solution)/shard_map/ppermute | solution.py:22
  589.4 2.0 copy-start.3
Sparse Core Ops, SparseCore 0:
  103.5 485.8 all-reduce.2
where the time goes:
time: 600 us; the launch traced here: 599 us
  waiting for transfers between devices  490 us (82%)
  starting transfers between devices  80.3 us (13%)
  between operations  14.6 us (2%)
    psum x1, waiting for transfers between devices, per_device(): lax.psum((grad_first, grad_second), ('lon', 'lat'))  484 us
    ppermute x6, starting transfers between devices, extended_2(): after = lax.ppermute(initial, axis, down)  39.9 us
    ppermute x6, starting transfers between devices, extended_2(): before = lax.ppermute(last, axis, up)  20.6 us
    ppermute x3, starting transfers between devices, shifted(): lax.ppermute(x, axis, [(i, (i + by) % devices) for i in range(devices)])  19.8 us
  transfers between devices with their start and end apart: 16, of which 5 were waited for; matrix products, arithmetic and copies ran while one was open for 1% of the time, Pallas kernels for 0%

commit v1 on v0

v1 whole, which is shorter than its diff:
```python
import math

import jax
import jax.numpy as jnp
from jax import lax
from jax.sharding import Mesh, PartitionSpec as P

LON = ("zh", "y")
LAT = ("x", "zl", "core")
SIZES = {"zh": 4, "y": 8, "x": 4, "zl": 3, "core": 2}
SCATTER = (("core", jnp.float32), (("y", "x"), jnp.bfloat16))
EXCHANGE = ("zh", "zl")


def swap(x, partner):
    lats, lons = lax.axis_size(LAT), lax.axis_size(LON)
    pairs = []
    for j in range(lons):
        for i in range(lats):
            to_lat, to_lon = partner(i, j)
            pairs.append((j * lats + i, (to_lon % lons) * lats + to_lat))
    return lax.ppermute(x, LON + LAT, pairs)


def halo_of_two(stack, north_pole, south_pole):
    lats, lons = lax.axis_size(LAT), lax.axis_size(LON)
    rows, cols = stack.shape[1:3]
    odd_row = lax.axis_index(LAT) % 2 == 1
    odd_col = lax.axis_index(LON) % 2 == 1

    def across_chips(i, j):
        to = i + 1 if i % 2 else i - 1
        return (to, j) if 0 <= to < lats else (i, j + lons // 2)

    top, bottom = stack[:, :2], stack[:, rows - 2 :]
    outer = swap(jnp.where(odd_row, bottom, top), across_chips)
    inner = swap(jnp.where(odd_row, top, bottom), lambda i, j: (i - 1 if i % 2 else i + 1, j))
    outer = jnp.where(north_pole | south_pole, outer[:, ::-1], outer)
    above = jnp.where(odd_row, inner, outer)
    below = jnp.where(odd_row, outer, inner)
    tall = jnp.concatenate([above, stack, below], axis=1)
    first, last = tall[:, :, :2], tall[:, :, cols - 2 :]
    far = swap(jnp.where(odd_col, last, first), lambda i, j: (i, j + 1 if j % 2 else j - 1))
    near = swap(jnp.where(odd_col, first, last), lambda i, j: (i, j - 1 if j % 2 else j + 1))
    left = jnp.where(odd_col, near, far)
    right = jnp.where(odd_col, far, near)
    return jnp.concatenate([left, tall, right], axis=2)


def tap_patches(padded):
    row_count, col_count = padded.shape[0] - 2, padded.shape[1] - 2
    return jnp.concatenate(
        [
            padded[tap_row : tap_row + row_count, tap_col : tap_col + col_count]
            for tap_row in range(3)
            for tap_col in range(3)
        ],
        axis=-1,
    )


def apply_kernel(patches, weight):
    return jnp.einsum(
        "rlk,kd->rld", patches, weight.reshape(-1, weight.shape[-1]), preferred_element_type=jnp.float32
    )


def outer_sums(patches, upstream):
    return jnp.einsum("rlk,rld->kd", patches, upstream, preferred_element_type=jnp.float32)


def turned(weight):
    return jnp.transpose(weight[::-1, ::-1], (0, 1, 3, 2))


def adjoint_rows(patches, weight, edge_rows, north_pole, south_pole):
    flipped = turned(weight)
    top = jnp.concatenate([jnp.where(north_pole, flipped[2:3], flipped[0:1]), flipped[1:]])
    bottom = jnp.concatenate([flipped[:2], jnp.where(south_pole, flipped[0:1], flipped[2:3])])
    return jnp.concatenate(
        [
            apply_kernel(patches[:edge_rows], top),
            apply_kernel(patches[edge_rows:-edge_rows], flipped),
            apply_kernel(patches[-edge_rows:], bottom),
        ]
    )


def all_sum(x):
    def exchange(v, axes):
        return lax.all_to_all(v, axes, 0, 0, tiled=True)

    def to_all(v, axes):
        return exchange(jnp.broadcast_to(v[None], (lax.axis_size(axes),) + v.shape), axes)

    piece = x
    for axes, dtype in SCATTER:
        pieces = piece.astype(dtype).reshape(lax.axis_size(axes), -1, x.shape[-1])
        piece = jnp.sum(exchange(pieces, axes).astype(jnp.float32), axis=0)
    piece = jnp.sum(to_all(piece, EXCHANGE), axis=0).astype(jnp.bfloat16)
    for axes, dtype in SCATTER[::-1]:
        piece = to_all(piece, axes).reshape(-1, x.shape[-1])
    return piece.astype(jnp.float32)


def per_device(fields, cotangent, weight_first, weight_second):
    row_count, col_count, channels = fields.shape
    lat_place = lax.axis_index(LAT)
    north_pole = lat_place == 0
    south_pole = lat_place == lax.axis_size(LAT) - 1
    extended = halo_of_two(jnp.stack([fields, cotangent]), north_pole, south_pole)

    patches_fields = tap_patches(extended[0])
    reversed_first = weight_first[::-1]
    first_sum = jnp.concatenate(
        [
            apply_kernel(patches_fields[:1], jnp.where(north_pole, reversed_first, weight_first)),
            apply_kernel(patches_fields[1:-1], weight_first),
            apply_kernel(patches_fields[-1:], jnp.where(south_pole, reversed_first, weight_first)),
        ]
    )
    hidden = jax.nn.silu(first_sum).astype(jnp.bfloat16)
    back_hidden = adjoint_rows(tap_patches(extended[1]), weight_second, 2, north_pole, south_pole)
    sigmoid_first = jax.nn.sigmoid(first_sum)
    back_first = (back_hidden * sigmoid_first * (1.0 + first_sum * (1.0 - sigmoid_first))).astype(
        jnp.bfloat16
    )
    patches_hidden = tap_patches(hidden)
    cells_total = row_count * lax.axis_size(LAT) * col_count * lax.axis_size(LON)
    grad_scale = 1.0 / math.sqrt(cells_total)
    grad_first = outer_sums(patches_fields[1:-1, 1:-1], back_first[1:-1, 1:-1])
    grad_second = outer_sums(patches_hidden, cotangent)
    grads = all_sum(jnp.concatenate([grad_first, grad_second])) * grad_scale
    grad_first, grad_second = (
        part.reshape(weight_first.shape) for part in jnp.split(grads, 2)
    )
    second_sum = apply_kernel(patches_hidden, weight_second)
    output = (fields.astype(jnp.float32) + second_sum).astype(jnp.bfloat16)
    back_fields = (
        cotangent.astype(jnp.float32)
        + adjoint_rows(tap_patches(back_first), weight_first, 1, north_pole, south_pole)
    ).astype(jnp.bfloat16)
    return (output, back_fields, grad_first, grad_second)


def solution(mesh):
    fine = Mesh(mesh.devices.reshape(tuple(SIZES.values())), tuple(SIZES))
    cells = P(LAT, LON, None)
    return jax.shard_map(
        per_device,
        mesh=fine,
        in_specs=(cells, cells, P(), P()),
        out_specs=(cells, cells, P(), P()),
        check_vma=False,
    )
```

time: 600 us -> 117 us (0.20)
  waiting for transfers between devices: 490 us -> 33.2 us
  starting transfers between devices: 80.3 us -> 40.8 us
  blocking collectives: 0 us -> 20.1 us
  between operations: 14.6 us -> 1.2 us
    psum x1 -> x0, waiting for transfers between devices: 484 us -> none  [per_device(): lax.psum((grad_first, grad_second), ('lon', 'lat'))]
    ppermute x15 -> x4, starting transfers between devices: 80.2 us -> 25.5 us  [swap(): return lax.ppermute(x, LON + LAT, pairs)]
    all_to_all x0 -> x3, waiting for transfers between devices: none -> 30.7 us  [exchange(): return lax.all_to_all(v, axes, 0, 0, tiled=True)]
    all_to_all x0 -> x2, blocking collectives: none -> 20.1 us  [exchange(): return lax.all_to_all(v, axes, 0, 0, tiled=True)]
    all_to_all x0 -> x3, starting transfers between devices: none -> 15.3 us  [exchange(): return lax.all_to_all(v, axes, 0, 0, tiled=True)]
  transfers between devices with their start and end apart: 16 -> 7, of which waited for: 5 -> 5; matrix products, arithmetic and copies ran while one was open for 1% -> 6% of each run, Pallas kernels for 0% -> 0%
where the time goes in v1:
time: 117 us; the launch traced here: 116 us
  starting transfers between devices  40.8 us (35%)
  waiting for transfers between devices  33.2 us (28%)
  blocking collectives  20.1 us (17%)
  local copies, waits for them, and re-layouts  9.29 us (8%)
  matrix products  6.56 us (6%)
  other arithmetic  4.99 us (4%)
  between operations  1.2 us (1%)
    all_to_all x3, waiting for transfers between devices, exchange(): return lax.all_to_all(v, axes, 0, 0, tiled=True)  30.7 us
    ppermute x4, starting transfers between devices, swap(): return lax.ppermute(x, LON + LAT, pairs)  25.5 us
    all_to_all x2, blocking collectives, exchange(): return lax.all_to_all(v, axes, 0, 0, tiled=True)  20.1 us
    all_to_all x3, starting transfers between devices, exchange(): return lax.all_to_all(v, axes, 0, 0, tiled=True)  15.3 us
    dot_general x10, matrix products, apply_kernel(): jnp.einsum('rlk,kd->rld', patches, weight.reshape(-1, weight.shape[-1]),...  5.51 us
    unnamed x50, local copies, waits for them, and re-layouts  4.4 us
    ppermute x4, waiting for transfers between devices, swap(): return lax.ppermute(x, LON + LAT, pairs)  2.57 us
  transfers between devices with their start and end apart: 7, of which 5 were waited for; matrix products, arithmetic and copies ran while one was open for 6% of the time, Pallas kernels for 0%

profile of v1, /device:TPU:1, one launch (start us, length us, event | category | flops | bytes accessed | tf_op | source)
XLA Modules:
  0.0 116.2 jit_solution(3698042686552737704)
XLA Ops:
  0.7 0.8 broadcast_select_fusion.10
  1.5 12.4 %collective-permute-start = (bf16[2,2,32,128]{3,2,1,0:T(8,128)(2,1)S(1)}, bf16[2,2,32,128]{3,2,1,0:T(8,128)(2,1)S(1)}, u32[]{:S(2)}, u32[]{:S(2)}) collective-permute-start(bf16[2,2,32,128]{3,2,1,0:T(8,128)(2,1)S(1)} %broadcast_select_fusion.11), channel_id=1, source_target_pairs={{0,1},{1,0},{2,3},{3,2},{4,5},{5,4},{6,7},{7,6},{8,9},{9,8},{10,11... | collective-permute-start | bytes 98312 | tf_op jit(solution)/shard_map/ppermute | solution.py:22
  13.9 1.9 %collective-permute-start.1 = (bf16[2,2,32,128]{3,2,1,0:T(8,128)(2,1)S(1)}, bf16[2,2,32,128]{3,2,1,0:T(8,128)(2,1)S(1)}, u32[]{:S(2)}, u32[]{:S(2)}) collective-permute-start(bf16[2,2,32,128]{3,2,1,0:T(8,128)(2,1)S(1)} %get-tuple-element.7), channel_id=1, source_target_pairs={{0,384},{1,2},{2,1},{3,4},{4,3},{5,6},{6,5},{7,8},{8,7},{9,10},{10... | collective-permute-start | bytes 98312 | tf_op jit(solution)/shard_map/ppermute | solution.py:22
  15.8 1.2 %copy.13 = bf16[3,3,128,128]{2,3,1,0:T(8,128)(2,1)S(1)} copy(bf16[3,3,128,128]{3,2,1,0:T(8,128)(2,1)} %param.6) | data formatting | bytes 589824 | tf_op args[2]
  17.4 0.6 copy-done
  18.4 0.8 collective-permute-done.1
  19.3 9.2 %collective-permute-start.3 = (bf16[2,20,2,128]{3,2,1,0:T(2,128)(2,1)S(1)}, bf16[2,20,2,128]{3,2,1,0:T(2,128)(2,1)S(1)}, u32[]{:S(2)}, u32[]{:S(2)}) collective-permute-start(bf16[2,20,2,128]{3,2,1,0:T(2,128)(2,1)S(1)} %bitcast.111), channel_id=1, source_target_pairs={{0,744},{1,745},{2,746},{3,747},{4,748},{5,749},{6,750},{7,751},{8... | collective-permute-start | bytes 61448 | tf_op jit(solution)/shard_map/ppermute | solution.py:22
  28.5 1.9 %collective-permute-start.2 = (bf16[2,20,2,128]{3,2,1,0:T(2,128)(2,1)S(1)}, bf16[2,20,2,128]{3,2,1,0:T(2,128)(2,1)S(1)}, u32[]{:S(2)}, u32[]{:S(2)}) collective-permute-start(bf16[2,20,2,128]{3,2,1,0:T(2,128)(2,1)S(1)} %get-tuple-element.4), channel_id=1, source_target_pairs={{0,24},{1,25},{2,26},{3,27},{4,28},{5,29},{6,30},{7,31},{8,32},{9,... | collective-permute-start | bytes 61448 | tf_op jit(solution)/shard_map/ppermute | solution.py:22
  30.4 0.7 pad_maximum_fusion.6
  31.2 1.8 %collective-permute-done.2 = bf16[2,20,2,128]{3,2,1,0:T(2,128)(2,1)S(1)} collective-permute-done((bf16[2,20,2,128]{3,2,1,0:T(2,128)(2,1)S(1)}, bf16[2,20,2,128]{3,2,1,0:T(2,128)(2,1)S(1)}, u32[]{:S(2)}, u32[]{:S(2)}) %collective-permute-start.2) | collective-permute-done | bytes 20512 | tf_op jit(solution)/shard_map/ppermute | solution.py:22
  35.0 0.5 fusion.11
  35.9 0.6 fusion.9
  36.7 0.5 convolution_bitcast_fusion.1
  37.8 0.5 convolution_bitcast_fusion
  38.3 0.5 copy-done.3
  38.9 11.6 %all_to_all.25 = f32[2,1152,128]{2,1,0:T(8,128)S(1)} all-to-all(f32[2,1152,128]{2,1,0:T(8,128)S(1)} %bitcast.86), channel_id=1, replica_groups=mesh['zh'=4,'y'=8,'x'=4,'zl'=3,'core'=2] {'core'}, dimensions={0} | all-to-all | bytes 2359296 | tf_op jit(solution)/shard_map/all_to_all | solution.py:91
  50.5 0.8 reduce_sum.27
  51.4 1.7 %convert_element_type.46 = bf16[32,36,128]{2,1,0:T(8,128)(2,1)} reshape(bf16[1152,128]{1,0:T(8,128)(2,1)} %reduce_sum.27) | data formatting | bytes 589824 | tf_op jit(solution)/shard_map/convert_element_type | solution.py:98
  53.1 3.9 %all-to-all-start.1 = ((bf16[32,36,128]{2,1,0:T(8,128)(2,1)}), bf16[32,36,128]{2,1,0:T(8,128)(2,1)S(1)}, u32[]{:S(2)}, u32[]{:S(2)}) async-start(bf16[32,36,128]{2,1,0:T(8,128)(2,1)} %convert_element_type.46), calls=%async_computation.1 | async-start | bytes 655360 | tf_op jit(solution)/shard_map/all_to_all | solution.py:91
  57.4 12.5 %all-to-all-done.1 = bf16[32,36,128]{2,1,0:T(8,128)(2,1)S(1)} async-done(((bf16[32,36,128]{2,1,0:T(8,128)(2,1)}), bf16[32,36,128]{2,1,0:T(8,128)(2,1)S(1)}, u32[]{:S(2)}, u32[]{:S(2)}) %all-to-all-start.1) | async-done | bytes 294944 | tf_op jit(solution)/shard_map/all_to_all | solution.py:91
  69.9 0.7 broadcast_in_dim.8
  70.6 4.2 %all-to-all-start.2 = ((f32[12,36,128]{2,1,0:T(8,128)}), f32[12,36,128]{2,1,0:T(8,128)}, u32[]{:S(2)}, u32[]{:S(2)}) async-start(f32[12,36,128]{2,1,0:T(8,128)} %broadcast_in_dim.8), calls=%async_computation.2 | async-start | bytes 491520 | tf_op jit(solution)/shard_map/all_to_all | solution.py:91
  75.1 1.1 fusion.13
  76.2 10.4 %all-to-all-done.2 = f32[12,36,128]{2,1,0:T(8,128)} async-done(((f32[12,36,128]{2,1,0:T(8,128)}), f32[12,36,128]{2,1,0:T(8,128)}, u32[]{:S(2)}, u32[]{:S(2)}) %all-to-all-start.2) | async-done | bytes 221216 | tf_op jit(solution)/shard_map/all_to_all | solution.py:91
  86.6 1.0 reduce_sum.29
  87.6 0.8 broadcast_in_dim.9
  88.4 7.2 %all-to-all-start.3 = ((bf16[32,36,128]{2,1,0:T(8,128)(2,1)}), bf16[32,36,128]{2,1,0:T(8,128)(2,1)S(1)}, u32[]{:S(2)}, u32[]{:S(2)}) async-start(bf16[32,36,128]{2,1,0:T(8,128)(2,1)} %broadcast_in_dim.9), calls=%async_computation.3 | async-start | bytes 655360 | tf_op jit(solution)/shard_map/all_to_all | solution.py:91
  95.8 0.7 fusion.4
  96.5 2.1 %fusion.1 = bf16[16,32,128]{2,1,0:T(8,128)(2,1)} fusion(bf16[16,32,1152]{2,1,0:T(8,128)(2,1)S(1)} %copy-done.4, bf16[1152,128,1]{1,0,2:T(8,128)(2,1)} %bitcast.99, bf16[16,32,128]{2,1,0:T(8,128)(2,1)S(1)} %copy-done.2), kind=kOutput, calls=%fused_computation.6 | convolution fusion | flops 151191552 | bytes 1736704 | tf_op jit(solution)/shard_map/rlk,kd->rld/dot_general | solution.py:63
  98.6 7.8 %all-to-all-done.3 = bf16[32,36,128]{2,1,0:T(8,128)(2,1)S(1)} async-done(((bf16[32,36,128]{2,1,0:T(8,128)(2,1)}), bf16[32,36,128]{2,1,0:T(8,128)(2,1)S(1)}, u32[]{:S(2)}, u32[]{:S(2)}) %all-to-all-start.3) | async-done | bytes 294944 | tf_op jit(solution)/shard_map/all_to_all | solution.py:91
  106.5 8.5 %all_to_all.26 = bf16[2,1152,128]{2,1,0:T(8,128)(2,1)S(1)} all-to-all(bf16[2,1152,128]{2,1,0:T(8,128)(2,1)S(1)} %broadcast_in_dim.22), channel_id=1, replica_groups=mesh['zh'=4,'y'=8,'x'=4,'zl'=3,'core'=2] {'core'}, dimensions={0} | all-to-all | bytes 1179648 | tf_op jit(solution)/shard_map/all_to_all | solution.py:91
  115.1 1.1 fusion.6
  (82 shorter events, 4.7 us)
Async XLA Ops:
  0.6 16.4 %copy-start.6 = (bf16[3,3,128,128]{3,2,1,0:T(8,128)(2,1)S(1)}, bf16[3,3,128,128]{3,2,1,0:T(8,128)(2,1)}, u32[]{:S(2)}) copy-start(bf16[3,3,128,128]{3,2,1,0:T(8,128)(2,1)} %param.7) | copy-start | bytes 884740
  1.5 16.9 %collective-permute-start = (bf16[2,2,32,128]{3,2,1,0:T(8,128)(2,1)S(1)}, bf16[2,2,32,128]{3,2,1,0:T(8,128)(2,1)S(1)}, u32[]{:S(2)}, u32[]{:S(2)}) collective-permute-start(bf16[2,2,32,128]{3,2,1,0:T(8,128)(2,1)S(1)} %broadcast_select_fusion.11), channel_id=1, source_target_pairs={{0,1},{1,0},{2,3},{3,2},{4,5},{5,4},{6,7},{7,6},{8,9},{9,8},{10,11... | collective-permute-start | bytes 98312 | tf_op jit(solution)/shard_map/ppermute | solution.py:22
  13.9 5.2 %collective-permute-start.1 = (bf16[2,2,32,128]{3,2,1,0:T(8,128)(2,1)S(1)}, bf16[2,2,32,128]{3,2,1,0:T(8,128)(2,1)S(1)}, u32[]{:S(2)}, u32[]{:S(2)}) collective-permute-start(bf16[2,2,32,128]{3,2,1,0:T(8,128)(2,1)S(1)} %get-tuple-element.7), channel_id=1, source_target_pairs={{0,384},{1,2},{2,1},{3,4},{4,3},{5,6},{6,5},{7,8},{8,7},{9,10},{10... | collective-permute-start | bytes 98312 | tf_op jit(solution)/shard_map/ppermute | solution.py:22
  17.0 1.0 copy-start
  18.2 1.0 copy-start.1
  18.2 1.0 copy-start.2
  19.3 12.0 %collective-permute-start.3 = (bf16[2,20,2,128]{3,2,1,0:T(2,128)(2,1)S(1)}, bf16[2,20,2,128]{3,2,1,0:T(2,128)(2,1)S(1)}, u32[]{:S(2)}, u32[]{:S(2)}) collective-permute-start(bf16[2,20,2,128]{3,2,1,0:T(2,128)(2,1)S(1)} %bitcast.111), channel_id=1, source_target_pairs={{0,744},{1,745},{2,746},{3,747},{4,748},{5,749},{6,750},{7,751},{8... | collective-permute-start | bytes 61448 | tf_op jit(solution)/shard_map/ppermute | solution.py:22
  28.5 4.5 %collective-permute-start.2 = (bf16[2,20,2,128]{3,2,1,0:T(2,128)(2,1)S(1)}, bf16[2,20,2,128]{3,2,1,0:T(2,128)(2,1)S(1)}, u32[]{:S(2)}, u32[]{:S(2)}) collective-permute-start(bf16[2,20,2,128]{3,2,1,0:T(2,128)(2,1)S(1)} %get-tuple-element.4), channel_id=1, source_target_pairs={{0,24},{1,25},{2,26},{3,27},{4,28},{5,29},{6,30},{7,31},{8,32},{9,... | collective-permute-start | bytes 61448 | tf_op jit(solution)/shard_map/ppermute | solution.py:22
  37.8 1.0 copy-start.3
  53.1 16.7 %all-to-all-start.1 = ((bf16[32,36,128]{2,1,0:T(8,128)(2,1)}), bf16[32,36,128]{2,1,0:T(8,128)(2,1)S(1)}, u32[]{:S(2)}, u32[]{:S(2)}) async-start(bf16[32,36,128]{2,1,0:T(8,128)(2,1)} %convert_element_type.46), calls=%async_computation.1 | async-start | bytes 655360 | tf_op jit(solution)/shard_map/all_to_all | solution.py:91
  70.6 16.0 %all-to-all-start.2 = ((f32[12,36,128]{2,1,0:T(8,128)}), f32[12,36,128]{2,1,0:T(8,128)}, u32[]{:S(2)}, u32[]{:S(2)}) async-start(f32[12,36,128]{2,1,0:T(8,128)} %broadcast_in_dim.8), calls=%async_computation.2 | async-start | bytes 491520 | tf_op jit(solution)/shard_map/all_to_all | solution.py:91
  75.0 20.6 %copy-start.5 = (bf16[3,3,128,128]{3,2,1,0:T(8,128)(2,1)S(1)}, bf16[3,3,128,128]{3,2,1,0:T(8,128)(2,1)}, u32[]{:S(2)}) copy-start(bf16[3,3,128,128]{3,2,1,0:T(8,128)(2,1)} %pad_maximum_fusion.6) | copy-start | bytes 884740
  76.2 19.6 %copy-start.7 = (f32[14,32,128]{2,1,0:T(8,128)S(1)}, f32[14,32,128]{2,1,0:T(8,128)}, u32[]{:S(2)}) copy-start(f32[14,32,128]{2,1,0:T(8,128)} %fusion.13) | copy-start | bytes 688132
  76.2 20.3 %copy-start.4 = (bf16[16,32,1152]{2,1,0:T(8,128)(2,1)S(1)}, bf16[16,32,1152]{2,1,0:T(8,128)(2,1)}, u32[]{:S(2)}) copy-start(bf16[16,32,1152]{2,1,0:T(8,128)(2,1)} %copy-done.3) | copy-start | bytes 3538948
  88.4 18.0 %all-to-all-start.3 = ((bf16[32,36,128]{2,1,0:T(8,128)(2,1)}), bf16[32,36,128]{2,1,0:T(8,128)(2,1)S(1)}, u32[]{:S(2)}, u32[]{:S(2)}) async-start(bf16[32,36,128]{2,1,0:T(8,128)(2,1)} %broadcast_in_dim.9), calls=%async_computation.3 | async-start | bytes 655360 | tf_op jit(solution)/shard_map/all_to_all | solution.py:91

commit v2 on v1

--- a/solution.py
+++ b/solution.py
@@ -5,10 +5,11 @@
 from jax import lax
 from jax.sharding import Mesh, PartitionSpec as P
 
+
 LON = ("zh", "y")
 LAT = ("x", "zl", "core")
 SIZES = {"zh": 4, "y": 8, "x": 4, "zl": 3, "core": 2}
-SCATTER = (("core", jnp.float32), (("y", "x"), jnp.bfloat16))
+SCATTER = ("y", "x")
 EXCHANGE = ("zh", "zl")
 
 
@@ -86,25 +87,34 @@
     )
 
 
-def all_sum(x):
+def all_sum(grad_first, grad_second):
     def exchange(v, axes):
         return lax.all_to_all(v, axes, 0, 0, tiled=True)
 
     def to_all(v, axes):
         return exchange(jnp.broadcast_to(v[None], (lax.axis_size(axes),) + v.shape), axes)
 
-    piece = x
-    for axes, dtype in SCATTER:
-        pieces = piece.astype(dtype).reshape(lax.axis_size(axes), -1, x.shape[-1])
-        piece = jnp.sum(exchange(pieces, axes).astype(jnp.float32), axis=0)
+    def other_core(v):
+        return lax.ppermute(v, "core", [(0, 1), (1, 0)])
+
+    rows, channels = grad_first.shape
+    low_core = lax.axis_index("core") == 0
+    kept = jnp.where(low_core, grad_first, grad_second)
+    given = jnp.where(low_core, grad_second, grad_first)
+    piece = (kept + other_core(given)).astype(jnp.bfloat16)
+    size = lax.axis_size(SCATTER)
+    piece = jnp.pad(piece, ((0, -rows % (8 * size)), (0, 0))).reshape(size, -1, channels)
+    piece = jnp.sum(exchange(piece, SCATTER).astype(jnp.float32), axis=0)
     piece = jnp.sum(to_all(piece, EXCHANGE), axis=0).astype(jnp.bfloat16)
-    for axes, dtype in SCATTER[::-1]:
-        piece = to_all(piece, axes).reshape(-1, x.shape[-1])
-    return piece.astype(jnp.float32)
+    half = to_all(piece, SCATTER).reshape(-1, channels)[:rows]
+    rest = other_core(half)
+    first = jnp.where(low_core, half, rest)
+    second = jnp.where(low_core, rest, half)
+    return first.astype(jnp.float32), second.astype(jnp.float32)
 
 
 def per_device(fields, cotangent, weight_first, weight_second):
-    row_count, col_count, channels = fields.shape
+    row_count, col_count, _ = fields.shape
     lat_place = lax.axis_index(LAT)
     north_pole = lat_place == 0
     south_pole = lat_place == lax.axis_size(LAT) - 1
@@ -130,9 +140,8 @@
     grad_scale = 1.0 / math.sqrt(cells_total)
     grad_first = outer_sums(patches_fields[1:-1, 1:-1], back_first[1:-1, 1:-1])
     grad_second = outer_sums(patches_hidden, cotangent)
-    grads = all_sum(jnp.concatenate([grad_first, grad_second])) * grad_scale
     grad_first, grad_second = (
-        part.reshape(weight_first.shape) for part in jnp.split(grads, 2)
+        (total * grad_scale).reshape(weight_first.shape) for total in all_sum(grad_first, grad_second)
     )
     second_sum = apply_kernel(patches_hidden, weight_second)
     output = (fields.astype(jnp.float32) + second_sum).astype(jnp.bfloat16)

time: 117 us -> 119 us (1.017)
  blocking collectives: 20.1 us -> 0 us
  starting transfers between devices: 40.8 us -> 55.9 us
  other arithmetic: 4.99 us -> 10.7 us
  matrix products: 6.56 us -> 9.5 us
  local copies, waits for them, and re-layouts: 9.29 us -> 6.67 us
  waiting for transfers between devices: 33.2 us -> 34.5 us
    all_to_all x2 -> x0, blocking collectives: 20.1 us -> none  [exchange(): return lax.all_to_all(v, axes, 0, 0, tiled=True)]
    ppermute x0 -> x2, starting transfers between devices: none -> 16 us  [other_core(): return lax.ppermute(v, 'core', [(0, 1), (1, 0)])]
    dot_general x10, matrix products: 5.51 us -> 7.43 us  [apply_kernel(): jnp.einsum('rlk,kd->rld', patches, weight.reshape(-1, weight.shape[-1]),...]
    concatenate x2, other arithmetic: 0.06 us -> 1.94 us  [adjoint_rows(): jnp.concatenate([jnp.where(north_pole, flipped[2:3], flipped[0:1]), flipp...]
    convert_element_type x1 -> x0, local copies, waits for them, and re-layouts: 1.74 us -> none  [all_sum(): pieces = piece.astype(dtype).reshape(lax.axis_size(axes), -1, x.shape[-1])]
    unnamed x50 -> x48, local copies, waits for them, and re-layouts: 4.4 us -> 3.24 us
  transfers between devices with their start and end apart: 7 -> 9, of which waited for: 5 -> 6; matrix products, arithmetic and copies ran while one was open for 6% -> 11% of each run, Pallas kernels for 0% -> 0%
where the time goes in v2:
time: 119 us; the launch traced here: 118 us
  starting transfers between devices  55.9 us (47%)
  waiting for transfers between devices  34.5 us (29%)
  other arithmetic  10.7 us (9%)
  matrix products  9.5 us (8%)
  local copies, waits for them, and re-layouts  6.67 us (6%)
    all_to_all x3, waiting for transfers between devices, exchange(): return lax.all_to_all(v, axes, 0, 0, tiled=True)  31.6 us
    ppermute x4, starting transfers between devices, swap(): return lax.ppermute(x, LON + LAT, pairs)  25.3 us
    ppermute x2, starting transfers between devices, other_core(): return lax.ppermute(v, 'core', [(0, 1), (1, 0)])  16 us
    all_to_all x3, starting transfers between devices, exchange(): return lax.all_to_all(v, axes, 0, 0, tiled=True)  14.6 us
    dot_general x10, matrix products, apply_kernel(): jnp.einsum('rlk,kd->rld', patches, weight.reshape(-1, weight.shape[-1]),...  7.43 us
    unnamed x48, local copies, waits for them, and re-layouts  3.24 us
  transfers between devices with their start and end apart: 9, of which 6 were waited for; matrix products, arithmetic and copies ran while one was open for 11% of the time, Pallas kernels for 0%

profile of v2, /device:TPU:1, one launch (start us, length us, event | category | flops | bytes accessed | tf_op | source)
XLA Modules:
  0.0 118.4 jit_solution(15108577650300711024)
XLA Ops:
  0.7 0.8 broadcast_select_fusion.11
  1.5 12.4 %collective-permute-start = (bf16[2,2,32,128]{3,2,1,0:T(8,128)(2,1)S(1)}, bf16[2,2,32,128]{3,2,1,0:T(8,128)(2,1)S(1)}, u32[]{:S(2)}, u32[]{:S(2)}) collective-permute-start(bf16[2,2,32,128]{3,2,1,0:T(8,128)(2,1)S(1)} %broadcast_select_fusion.12), channel_id=1, source_target_pairs={{0,1},{1,0},{2,3},{3,2},{4,5},{5,4},{6,7},{7,6},{8,9},{9,8},{10,11... | collective-permute-start | bytes 98312 | tf_op jit(solution)/shard_map/ppermute | solution.py:23
  13.9 1.9 %collective-permute-start.1 = (bf16[2,2,32,128]{3,2,1,0:T(8,128)(2,1)S(1)}, bf16[2,2,32,128]{3,2,1,0:T(8,128)(2,1)S(1)}, u32[]{:S(2)}, u32[]{:S(2)}) collective-permute-start(bf16[2,2,32,128]{3,2,1,0:T(8,128)(2,1)S(1)} %get-tuple-element.7), channel_id=1, source_target_pairs={{0,384},{1,2},{2,1},{3,4},{4,3},{5,6},{6,5},{7,8},{8,7},{9,10},{10... | collective-permute-start | bytes 98312 | tf_op jit(solution)/shard_map/ppermute | solution.py:23
  15.8 1.2 copy.12
  17.0 0.7 fusion.7
  20.4 9.1 %collective-permute-start.3 = (bf16[2,20,2,128]{3,2,1,0:T(2,128)(2,1)}, bf16[2,20,2,128]{3,2,1,0:T(2,128)(2,1)}, u32[]{:S(2)}, u32[]{:S(2)}) collective-permute-start(bf16[2,20,2,128]{3,2,1,0:T(2,128)(2,1)} %bitcast.82), channel_id=1, source_target_pairs={{0,744},{1,745},{2,746},{3,747},{4,748},{5,749},{6,750},{7,751},{8... | collective-permute-start | bytes 61448 | tf_op jit(solution)/shard_map/ppermute | solution.py:23
  29.5 1.9 %collective-permute-start.2 = (bf16[2,20,2,128]{3,2,1,0:T(2,128)(2,1)}, bf16[2,20,2,128]{3,2,1,0:T(2,128)(2,1)}, u32[]{:S(2)}, u32[]{:S(2)}) collective-permute-start(bf16[2,20,2,128]{3,2,1,0:T(2,128)(2,1)} %get-tuple-element.4), channel_id=1, source_target_pairs={{0,24},{1,25},{2,26},{3,27},{4,28},{5,29},{6,30},{7,31},{8,32},{9,... | collective-permute-start | bytes 61448 | tf_op jit(solution)/shard_map/ppermute | solution.py:23
  31.4 1.1 pad_maximum_fusion.2
  32.6 1.8 %collective-permute-done.2 = bf16[2,20,2,128]{3,2,1,0:T(2,128)(2,1)} collective-permute-done((bf16[2,20,2,128]{3,2,1,0:T(2,128)(2,1)}, bf16[2,20,2,128]{3,2,1,0:T(2,128)(2,1)}, u32[]{:S(2)}, u32[]{:S(2)}) %collective-permute-start.2) | collective-permute-done | bytes 20512 | tf_op jit(solution)/shard_map/ppermute | solution.py:23
  34.3 0.8 broadcast_select_fusion.6
  35.1 1.0 pad_maximum_fusion
  40.6 1.5 %broadcast_select_fusion = (f32[1152,128]{1,0:T(8,128)}, f32[1152,128]{1,0:T(8,128)}) fusion(f32[1152,128]{1,0:T(8,128)S(1)} %convolution_bitcast_fusion.1, pred[]{:T(512)S(6)} %eq.22, bf16[16,32,1152]{2,1,0:T(8,128)(2,1)S(1)} %slice_dynamic-update-slice_fusion.26, bf16[16,32,128]{2,1,0:T(8,128)(2,1)S(1)} %copy-done.1), kind=kOutput, calls=%fused_computation.26 | convolution fusion | flops 151142400 | bytes 3080193 | tf_op jit(solution)/shard_map/rlk,rld->kd/dot_general | solution.py:70
  42.1 9.4 %collective-permute-start.4 = (f32[1152,128]{1,0:T(8,128)}, f32[1152,128]{1,0:T(8,128)}, u32[]{:S(2)}, u32[]{:S(2)}) collective-permute-start(f32[1152,128]{1,0:T(8,128)} %get-tuple-element.30), channel_id=1, source_target_pairs={{0,1},{1,0},{2,3},{3,2},{4,5},{5,4},{6,7},{7,6},{8,9},{9,8},{10,11... | collective-permute-start | bytes 1769480 | tf_op jit(solution)/shard_map/ppermute | solution.py:98
  51.5 0.9 pad_maximum_fusion.4
  52.5 0.9 collective-permute-done.4
  53.4 1.2 add_convert_fusion
  54.6 0.7 pad.4
  55.3 3.9 %all-to-all-start = ((bf16[32,40,128]{2,1,0:T(8,128)(2,1)}), bf16[32,40,128]{2,1,0:T(8,128)(2,1)S(1)}, u32[]{:S(2)}, u32[]{:S(2)}) async-start(bf16[32,40,128]{2,1,0:T(8,128)(2,1)} %bitcast.32), calls=%async_computation | async-start | bytes 655360 | tf_op jit(solution)/shard_map/all_to_all | solution.py:92
  59.4 12.7 %all-to-all-done = bf16[32,40,128]{2,1,0:T(8,128)(2,1)S(1)} async-done(((bf16[32,40,128]{2,1,0:T(8,128)(2,1)}), bf16[32,40,128]{2,1,0:T(8,128)(2,1)S(1)}, u32[]{:S(2)}, u32[]{:S(2)}) %all-to-all-start) | async-done | bytes 327712 | tf_op jit(solution)/shard_map/all_to_all | solution.py:92
  72.1 0.7 broadcast_in_dim.4
  72.8 3.5 %all-to-all-start.1 = ((f32[12,40,128]{2,1,0:T(8,128)}), f32[12,40,128]{2,1,0:T(8,128)S(1)}, u32[]{:S(2)}, u32[]{:S(2)}) async-start(f32[12,40,128]{2,1,0:T(8,128)} %broadcast_in_dim.4), calls=%async_computation.1 | async-start | bytes 491520 | tf_op jit(solution)/shard_map/all_to_all | solution.py:92
  76.6 11.6 %all-to-all-done.1 = f32[12,40,128]{2,1,0:T(8,128)S(1)} async-done(((f32[12,40,128]{2,1,0:T(8,128)}), f32[12,40,128]{2,1,0:T(8,128)S(1)}, u32[]{:S(2)}, u32[]{:S(2)}) %all-to-all-start.1) | async-done | bytes 245792 | tf_op jit(solution)/shard_map/all_to_all | solution.py:92
  88.2 0.8 broadcast_in_dim.5
  88.9 7.2 %all-to-all-start.2 = ((bf16[32,40,128]{2,1,0:T(8,128)(2,1)}), bf16[32,40,128]{2,1,0:T(8,128)(2,1)S(1)}, u32[]{:S(2)}, u32[]{:S(2)}) async-start(bf16[32,40,128]{2,1,0:T(8,128)(2,1)} %broadcast_in_dim.5), calls=%async_computation.2 | async-start | bytes 655360 | tf_op jit(solution)/shard_map/all_to_all | solution.py:92
  96.2 1.1 convolution_bitcast_fusion.5
  97.4 1.1 convolution_bitcast_fusion.4
  98.5 1.1 fusion.12
  99.6 7.3 %all-to-all-done.2 = bf16[32,40,128]{2,1,0:T(8,128)(2,1)S(1)} async-done(((bf16[32,40,128]{2,1,0:T(8,128)(2,1)}), bf16[32,40,128]{2,1,0:T(8,128)(2,1)S(1)}, u32[]{:S(2)}, u32[]{:S(2)}) %all-to-all-start.2) | async-done | bytes 327712 | tf_op jit(solution)/shard_map/all_to_all | solution.py:92
  106.9 6.6 %collective-permute-start.5 = (bf16[1152,128]{1,0:T(8,128)(2,1)S(1)}, bf16[1152,128]{1,0:T(8,128)(2,1)S(1)}, u32[]{:S(2)}, u32[]{:S(2)}) collective-permute-start(bf16[1152,128]{1,0:T(8,128)(2,1)S(1)} %slice.300), channel_id=1, source_target_pairs={{0,1},{1,0},{2,3},{3,2},{4,5},{5,4},{6,7},{7,6},{8,9},{9,8},{10,11... | collective-permute-start | bytes 884744 | tf_op jit(solution)/shard_map/ppermute | solution.py:98
  113.6 1.6 %fusion.4 = bf16[16,32,128]{2,1,0:T(8,128)(2,1)} fusion(f32[1,32,128]{2,1,0:T(8,128)S(1)} %convolution_bitcast_fusion.4, f32[14,32,128]{2,1,0:T(8,128)} %fusion.12, f32[1,32,128]{2,1,0:T(8,128)S(1)} %convolution_bitcast_fusion.5, bf16[16,32,128]{2,1,0:T(8,128)(2,1)S(1)} %copy-done.1), kind=kLoop, calls=%fused_computation.28 | loop fusion | flops 327680 | bytes 524288 | tf_op jit(solution)/shard_map/convert_element_type | solution.py:151
  115.2 2.1 %fusion.1 = bf16[16,32,128]{2,1,0:T(8,128)(2,1)} fusion(bf16[16,32,1152]{2,1,0:T(8,128)(2,1)S(1)} %slice_dynamic-update-slice_fusion.26, bf16[1152,128,1]{1,0,2:T(8,128)(2,1)} %bitcast.97, bf16[16,32,128]{2,1,0:T(8,128)(2,1)S(1)} %copy-done.2), kind=kOutput, calls=%fused_computation.4 | convolution fusion | flops 151191552 | bytes 1736704 | tf_op jit(solution)/shard_map/rlk,kd->rld/dot_general | solution.py:64
  117.3 1.1 convert_multiply_fusion
  (78 shorter events, 7.6 us)
Async XLA Ops:
  0.6 17.1 %copy-start = (bf16[3,3,128,128]{3,2,1,0:T(8,128)(2,1)S(1)}, bf16[3,3,128,128]{3,2,1,0:T(8,128)(2,1)}, u32[]{:S(2)}) copy-start(bf16[3,3,128,128]{3,2,1,0:T(8,128)(2,1)} %param.6) | copy-start | bytes 884740
  1.5 17.4 %collective-permute-start = (bf16[2,2,32,128]{3,2,1,0:T(8,128)(2,1)S(1)}, bf16[2,2,32,128]{3,2,1,0:T(8,128)(2,1)S(1)}, u32[]{:S(2)}, u32[]{:S(2)}) collective-permute-start(bf16[2,2,32,128]{3,2,1,0:T(8,128)(2,1)S(1)} %broadcast_select_fusion.12), channel_id=1, source_target_pairs={{0,1},{1,0},{2,3},{3,2},{4,5},{5,4},{6,7},{7,6},{8,9},{9,8},{10,11... | collective-permute-start | bytes 98312 | tf_op jit(solution)/shard_map/ppermute | solution.py:23
  13.9 5.2 %collective-permute-start.1 = (bf16[2,2,32,128]{3,2,1,0:T(8,128)(2,1)S(1)}, bf16[2,2,32,128]{3,2,1,0:T(8,128)(2,1)S(1)}, u32[]{:S(2)}, u32[]{:S(2)}) collective-permute-start(bf16[2,2,32,128]{3,2,1,0:T(8,128)(2,1)S(1)} %get-tuple-element.7), channel_id=1, source_target_pairs={{0,384},{1,2},{2,1},{3,4},{4,3},{5,6},{6,5},{7,8},{8,7},{9,10},{10... | collective-permute-start | bytes 98312 | tf_op jit(solution)/shard_map/ppermute | solution.py:23
  17.8 1.4 %copy-start.1 = (bf16[16,32,128]{2,1,0:T(8,128)(2,1)S(1)}, bf16[16,32,128]{2,1,0:T(8,128)(2,1)}, u32[]{:S(2)}) copy-start(bf16[16,32,128]{2,1,0:T(8,128)(2,1)} %param.5) | copy-start | bytes 393220
  17.8 1.4 %copy-start.2 = (bf16[16,32,128]{2,1,0:T(8,128)(2,1)S(1)}, bf16[16,32,128]{2,1,0:T(8,128)(2,1)}, u32[]{:S(2)}) copy-start(bf16[16,32,128]{2,1,0:T(8,128)(2,1)} %param.4) | copy-start | bytes 393220
  19.2 12.3 %copy-start.6 = (bf16[2,2,32,128]{3,2,1,0:T(8,128)(2,1)}, bf16[2,2,32,128]{3,2,1,0:T(8,128)(2,1)S(1)}, u32[]{:S(2)}) copy-start(bf16[2,2,32,128]{3,2,1,0:T(8,128)(2,1)S(1)} %get-tuple-element.27) | copy-start | bytes 98308
  20.4 12.1 %collective-permute-start.3 = (bf16[2,20,2,128]{3,2,1,0:T(2,128)(2,1)}, bf16[2,20,2,128]{3,2,1,0:T(2,128)(2,1)}, u32[]{:S(2)}, u32[]{:S(2)}) collective-permute-start(bf16[2,20,2,128]{3,2,1,0:T(2,128)(2,1)} %bitcast.82), channel_id=1, source_target_pairs={{0,744},{1,745},{2,746},{3,747},{4,748},{5,749},{6,750},{7,751},{8... | collective-permute-start | bytes 61448 | tf_op jit(solution)/shard_map/ppermute | solution.py:23
  29.5 4.8 %collective-permute-start.2 = (bf16[2,20,2,128]{3,2,1,0:T(2,128)(2,1)}, bf16[2,20,2,128]{3,2,1,0:T(2,128)(2,1)}, u32[]{:S(2)}, u32[]{:S(2)}) collective-permute-start(bf16[2,20,2,128]{3,2,1,0:T(2,128)(2,1)} %get-tuple-element.4), channel_id=1, source_target_pairs={{0,24},{1,25},{2,26},{3,27},{4,28},{5,29},{6,30},{7,31},{8,32},{9,... | collective-permute-start | bytes 61448 | tf_op jit(solution)/shard_map/ppermute | solution.py:23
  40.1 2.0 %copy-start.3 = (f32[1152,128]{1,0:T(8,128)}, f32[1152,128]{1,0:T(8,128)S(1)}, u32[]{:S(2)}) copy-start(f32[1152,128]{1,0:T(8,128)S(1)} %convolution_bitcast_fusion.1) | copy-start | bytes 1769476
  42.1 11.3 %collective-permute-start.4 = (f32[1152,128]{1,0:T(8,128)}, f32[1152,128]{1,0:T(8,128)}, u32[]{:S(2)}, u32[]{:S(2)}) collective-permute-start(f32[1152,128]{1,0:T(8,128)} %get-tuple-element.30), channel_id=1, source_target_pairs={{0,1},{1,0},{2,3},{3,2},{4,5},{5,4},{6,7},{7,6},{8,9},{9,8},{10,11... | collective-permute-start | bytes 1769480 | tf_op jit(solution)/shard_map/ppermute | solution.py:98
  51.5 1.9 %copy-start.4 = (f32[1152,128]{1,0:T(8,128)S(1)}, f32[1152,128]{1,0:T(8,128)}, u32[]{:S(2)}) copy-start(f32[1152,128]{1,0:T(8,128)} %copy-done.3) | copy-start | bytes 1769476
  51.5 1.9 %copy-start.5 = (f32[1152,128]{1,0:T(8,128)S(1)}, f32[1152,128]{1,0:T(8,128)}, u32[]{:S(2)}) copy-start(f32[1152,128]{1,0:T(8,128)} %get-tuple-element.31) | copy-start | bytes 1769476
  55.3 16.7 %all-to-all-start = ((bf16[32,40,128]{2,1,0:T(8,128)(2,1)}), bf16[32,40,128]{2,1,0:T(8,128)(2,1)S(1)}, u32[]{:S(2)}, u32[]{:S(2)}) async-start(bf16[32,40,128]{2,1,0:T(8,128)(2,1)} %bitcast.32), calls=%async_computation | async-start | bytes 655360 | tf_op jit(solution)/shard_map/all_to_all | solution.py:92
  72.8 15.3 %all-to-all-start.1 = ((f32[12,40,128]{2,1,0:T(8,128)}), f32[12,40,128]{2,1,0:T(8,128)S(1)}, u32[]{:S(2)}, u32[]{:S(2)}) async-start(f32[12,40,128]{2,1,0:T(8,128)} %broadcast_in_dim.4), calls=%async_computation.1 | async-start | bytes 491520 | tf_op jit(solution)/shard_map/all_to_all | solution.py:92
  88.9 18.0 %all-to-all-start.2 = ((bf16[32,40,128]{2,1,0:T(8,128)(2,1)}), bf16[32,40,128]{2,1,0:T(8,128)(2,1)S(1)}, u32[]{:S(2)}, u32[]{:S(2)}) async-start(bf16[32,40,128]{2,1,0:T(8,128)(2,1)} %broadcast_in_dim.5), calls=%async_computation.2 | async-start | bytes 655360 | tf_op jit(solution)/shard_map/all_to_all | solution.py:92
  106.9 10.3 %collective-permute-start.5 = (bf16[1152,128]{1,0:T(8,128)(2,1)S(1)}, bf16[1152,128]{1,0:T(8,128)(2,1)S(1)}, u32[]{:S(2)}, u32[]{:S(2)}) collective-permute-start(bf16[1152,128]{1,0:T(8,128)(2,1)S(1)} %slice.300), channel_id=1, source_target_pairs={{0,1},{1,0},{2,3},{3,2},{4,5},{5,4},{6,7},{7,6},{8,9},{9,8},{10,11... | collective-permute-start | bytes 884744 | tf_op jit(solution)/shard_map/ppermute | solution.py:98

commit v3 on v2

v3 whole, which is shorter than its diff:
```python
import math

import jax
import jax.numpy as jnp
from jax import lax
from jax.experimental import pallas as pl
from jax.experimental.pallas import tpu as pltpu
from jax.sharding import Mesh, PartitionSpec as P


LON = ("zh", "y")
LAT = ("x", "zl", "core")
SIZES = {"zh": 4, "y": 8, "x": 4, "zl": 3, "core": 2}
SCATTER = ("y", "x")
EXCHANGE = ("zh", "zl")


def swap(x, partner):
    lats, lons = lax.axis_size(LAT), lax.axis_size(LON)
    pairs = []
    for j in range(lons):
        for i in range(lats):
            to_lat, to_lon = partner(i, j)
            pairs.append((j * lats + i, (to_lon % lons) * lats + to_lat))
    return lax.ppermute(x, LON + LAT, pairs)


def halo_of_two(stack, north_pole, south_pole):
    lats, lons = lax.axis_size(LAT), lax.axis_size(LON)
    rows, cols = stack.shape[1:3]
    odd_row = lax.axis_index(LAT) % 2 == 1
    odd_col = lax.axis_index(LON) % 2 == 1

    def across_chips(i, j):
        to = i + 1 if i % 2 else i - 1
        return (to, j) if 0 <= to < lats else (i, j + lons // 2)

    top, bottom = stack[:, :2], stack[:, rows - 2 :]
    outer = swap(jnp.where(odd_row, bottom, top), across_chips)
    inner = swap(jnp.where(odd_row, top, bottom), lambda i, j: (i - 1 if i % 2 else i + 1, j))
    outer = jnp.where(north_pole | south_pole, outer[:, ::-1], outer)
    above = jnp.where(odd_row, inner, outer)
    below = jnp.where(odd_row, outer, inner)
    tall = jnp.concatenate([above, stack, below], axis=1)
    first, last = tall[:, :, :2], tall[:, :, cols - 2 :]
    far = swap(jnp.where(odd_col, last, first), lambda i, j: (i, j + 1 if j % 2 else j - 1))
    near = swap(jnp.where(odd_col, first, last), lambda i, j: (i, j - 1 if j % 2 else j + 1))
    left = jnp.where(odd_col, near, far).astype(jnp.float32)
    right = jnp.where(odd_col, far, near).astype(jnp.float32)
    return above, below, left, right


def conv_rows(taps_ref, start, count, weight_ref, order):
    total = None
    for tap_row, kernel_row in enumerate(order):
        taps = taps_ref[start + tap_row : start + tap_row + count]
        term = jnp.dot(
            taps.reshape(-1, taps.shape[-1]),
            weight_ref[kernel_row],
            preferred_element_type=jnp.float32,
        )
        total = term if total is None else total + term
    return total.reshape(count, -1, total.shape[-1])


def outer_rows(taps_ref, tap_row, rows, upstream):
    taps = taps_ref[tap_row : tap_row + rows]
    return lax.dot_general(
        taps.reshape(-1, taps.shape[-1]),
        upstream,
        (((0,), (0,)), ((), ())),
        preferred_element_type=jnp.float32,
    )


def ring_kernel(
    flags, fields, cotangent, above, below, left, right, first, turned_second,
    ring, kept, given,
    padded, taps, sums, gates, hidden_taps, field_taps,
):
    rows, cols, channels = fields.shape
    wide = ring.shape[2]
    north, south, low = flags[0] == 1, flags[1] == 1, flags[2] == 1
    for which, own in enumerate((fields, cotangent)):
        padded[which, :, cols:] = jnp.zeros((rows + 4, padded.shape[2] - cols, channels), jnp.float32)
        padded[which, :2, 8 : 8 + cols] = above[which].astype(jnp.float32)
        padded[which, 2 : 2 + rows, 8 : 8 + cols] = own[...].astype(jnp.float32)
        padded[which, 2 + rows :, 8 : 8 + cols] = below[which].astype(jnp.float32)
        padded[which, :, 6:8] = left[which]
        padded[which, :, 8 + cols : 10 + cols] = right[which]
        for tap in range(3):
            taps[which, :, :, channels * tap : channels * (tap + 1)] = padded[
                which, :, 6 + tap : 6 + tap + wide
            ].astype(jnp.bfloat16)
    for tap in range(3):
        field_taps[:, :, channels * tap : channels * (tap + 1)] = padded[
            0, 1 : 3 + rows, 7 + tap : 7 + tap + cols
        ].astype(jnp.bfloat16)
    of_fields, of_cotangent = taps.at[0], taps.at[1]
    sums[0] = conv_rows(of_fields, 0, rows + 2, first, (0, 1, 2))
    sums[1] = conv_rows(of_cotangent, 0, rows + 2, turned_second, (0, 1, 2))

    @pl.when(north)
    def _():
        sums[0, :1] = conv_rows(of_fields, 0, 1, first, (2, 1, 0))
        sums[1, :2] = conv_rows(of_cotangent, 0, 2, turned_second, (2, 1, 2))

    @pl.when(south)
    def _():
        sums[0, rows + 1 :] = conv_rows(of_fields, rows + 1, 1, first, (2, 1, 0))
        sums[1, rows:] = conv_rows(of_cotangent, rows, 2, turned_second, (0, 1, 0))

    first_sum = sums[0]
    gate = jax.nn.sigmoid(first_sum)
    hidden = first_sum * gate
    back_first = sums[1] * gate * (1.0 + first_sum * (1.0 - gate))
    gates[0] = hidden
    gates[1] = back_first
    ring[0] = hidden.astype(jnp.bfloat16)
    ring[1] = back_first.astype(jnp.bfloat16)
    for tap in range(3):
        hidden_taps[:, :, channels * tap : channels * (tap + 1)] = gates[
            0, :, tap : tap + cols
        ].astype(jnp.bfloat16)
    own_back = gates[1, 1 : 1 + rows, 1 : 1 + cols].astype(jnp.bfloat16).reshape(-1, channels)
    own_cotangent = cotangent[...].reshape(-1, channels)
    spare = kept.shape[0] - 9 * channels
    if spare:
        kept[9 * channels :] = jnp.zeros((spare, channels), jnp.float32)
        given[9 * channels :] = jnp.zeros((spare, channels), jnp.float32)
    for tap_row in range(3):
        grad_first = outer_rows(field_taps, tap_row, rows, own_back)
        grad_second = outer_rows(hidden_taps, tap_row, rows, own_cotangent)
        place = slice(3 * channels * tap_row, 3 * channels * (tap_row + 1))

        @pl.when(low)
        def _():
            kept[place] = grad_first
            given[place] = grad_second

        @pl.when(jnp.logical_not(low))
        def _():
            kept[place] = grad_second
            given[place] = grad_first


def output_kernel(flags, ring, fields, cotangent, second, turned_first, output, back_fields, wide_ring, taps, sums):
    rows, cols, channels = fields.shape
    north, south = flags[0] == 1, flags[1] == 1
    for which in range(2):
        wide_ring[which] = ring[which].astype(jnp.float32)
        for tap in range(3):
            taps[which, :, :, channels * tap : channels * (tap + 1)] = wide_ring[
                which, :, tap : tap + cols
            ].astype(jnp.bfloat16)
    second_sum = conv_rows(taps.at[0], 0, rows, second, (0, 1, 2))
    output[...] = (fields[...].astype(jnp.float32) + second_sum).astype(jnp.bfloat16)
    of_back = taps.at[1]
    sums[...] = conv_rows(of_back, 0, rows, turned_first, (0, 1, 2))

    @pl.when(north)
    def _():
        sums[:1] = conv_rows(of_back, 0, 1, turned_first, (2, 1, 2))

    @pl.when(south)
    def _():
        sums[rows - 1 :] = conv_rows(of_back, rows - 1, 1, turned_first, (0, 1, 0))

    back_fields[...] = (cotangent[...].astype(jnp.float32) + sums[...]).astype(jnp.bfloat16)


def call(kernel, out_shapes, scratch, flops, *operands):
    vmem = pl.BlockSpec(memory_space=pltpu.VMEM)
    moved = sum(math.prod(v.shape) * v.dtype.itemsize for v in (*operands, *out_shapes))
    return pl.pallas_call(
        kernel,
        out_shape=out_shapes,
        in_specs=[pl.BlockSpec(memory_space=pltpu.SMEM)] + [vmem] * (len(operands) - 1),
        out_specs=[vmem] * len(out_shapes),
        scratch_shapes=[pltpu.VMEM(shape, dtype) for shape, dtype in scratch],
        compiler_params=pltpu.CompilerParams(vmem_limit_bytes=24 * 2**20),
        cost_estimate=pl.CostEstimate(flops=flops, bytes_accessed=moved, transcendentals=0),
    )(*operands)


def turned(weight):
    return jnp.transpose(weight[::-1, ::-1], (0, 1, 3, 2))


def by_row(weight):
    return weight.reshape(weight.shape[0], -1, weight.shape[-1])


def all_sum(kept, given, finish, operands):
    def exchange(v, axes):
        return lax.all_to_all(v, axes, 0, 0, tiled=True)

    def to_all(v, axes):
        return exchange(jnp.broadcast_to(v[None], (lax.axis_size(axes),) + v.shape), axes)

    def other_core(v):
        return lax.ppermute(v, "core", [(0, 1), (1, 0)])

    channels = kept.shape[-1]
    piece = (kept + other_core(given)).astype(jnp.bfloat16)
    piece, operands = lax.optimization_barrier((piece, operands))
    outputs = finish(*operands)
    piece = piece.reshape(lax.axis_size(SCATTER), -1, channels)
    piece = jnp.sum(exchange(piece, SCATTER).astype(jnp.float32), axis=0)
    piece = jnp.sum(to_all(piece, EXCHANGE), axis=0).astype(jnp.bfloat16)
    half = to_all(piece, SCATTER).reshape(-1, channels)[: 9 * channels]
    half, outputs = lax.optimization_barrier((half, outputs))
    return half, other_core(half), outputs


def per_device(fields, cotangent, weight_first, weight_second):
    rows, cols, channels = fields.shape
    lat_place = lax.axis_index(LAT)
    north_pole = lat_place == 0
    south_pole = lat_place == lax.axis_size(LAT) - 1
    low_core = lax.axis_index("core") == 0
    flags = jnp.stack([north_pole, south_pole, low_core, low_core]).astype(jnp.int32)
    edges = halo_of_two(jnp.stack([fields, cotangent]), north_pole, south_pole)
    wide = -(-(cols + 2) // 16) * 16
    taps = 3 * channels
    flops = 2 * rows * cols * channels * channels * 9
    split = 8 * lax.axis_size(SCATTER)
    half = jax.ShapeDtypeStruct((-(-9 * channels // split) * split, channels), jnp.float32)
    bf16, f32 = jnp.bfloat16, jnp.float32
    ring, kept, given = call(
        ring_kernel,
        (jax.ShapeDtypeStruct((2, rows + 2, wide, channels), bf16), half, half),
        (
            ((2, rows + 4, wide + 8, channels), f32),
            ((2, rows + 4, wide, taps), bf16),
            ((2, rows + 2, wide, channels), f32),
            ((2, rows + 2, wide, channels), f32),
            ((rows + 2, cols, taps), bf16),
            ((rows + 2, cols, taps), bf16),
        ),
        4 * flops,
        flags, fields, cotangent, *edges, by_row(weight_first), by_row(turned(weight_second)),
    )
    block = jax.ShapeDtypeStruct(fields.shape, bf16)

    def finish(*operands):
        return call(
            output_kernel,
            (block, block),
            (
                ((2, rows + 2, wide, channels), f32),
                ((2, rows + 2, cols, taps), bf16),
                ((rows, cols, channels), f32),
            ),
            2 * flops,
            *operands,
        )

    mine, theirs, (output, back_fields) = all_sum(
        kept,
        given,
        finish,
        (flags, ring, fields, cotangent, by_row(weight_second), by_row(turned(weight_first))),
    )
    cells_total = rows * lax.axis_size(LAT) * cols * lax.axis_size(LON)
    grad_scale = 1.0 / math.sqrt(cells_total)
    grad_first, grad_second = (
        (jnp.where(low_core, one, other).astype(f32) * grad_scale).reshape(weight_first.shape)
        for one, other in ((mine, theirs), (theirs, mine))
    )
    return (output, back_fields, grad_first, grad_second)


def solution(mesh):
    fine = Mesh(mesh.devices.reshape(tuple(SIZES.values())), tuple(SIZES))
    cells = P(LAT, LON, None)
    return jax.shard_map(
        per_device,
        mesh=fine,
        in_specs=(cells, cells, P(), P()),
        out_specs=(cells, cells, P(), P()),
        check_vma=False,
    )
```

time: 119 us -> 111 us (0.933)
  blocking collectives: 0 us -> 34.7 us
  waiting for transfers between devices: 34.5 us -> 15.6 us
  matrix products: 9.5 us -> 0 us
  other arithmetic: 10.7 us -> 3.37 us
  starting transfers between devices: 55.9 us -> 48.8 us
  Pallas kernels: 0 us -> 5.41 us
  local copies, waits for them, and re-layouts: 6.67 us -> 1.3 us
    all_to_all x0 -> x2, blocking collectives: none -> 34.7 us  [exchange(): return lax.all_to_all(v, axes, 0, 0, tiled=True)]
    all_to_all x3 -> x1, waiting for transfers between devices: 31.6 us -> 8.73 us  [exchange(): return lax.all_to_all(v, axes, 0, 0, tiled=True)]
    dot_general x12 -> x0, matrix products: 9.5 us -> none  [the longest x10 7.43 us: apply_kernel(): jnp.einsum('rlk,kd->rld', patches, weight.reshape(-1, weight.shape[-1]),...]
    all_to_all x3 -> x1, starting transfers between devices: 14.6 us -> 6.41 us  [exchange(): return lax.all_to_all(v, axes, 0, 0, tiled=True)]
    pallas_call x0 -> x2, Pallas kernels: none -> 5.41 us  [call(): pl.pallas_call(kernel, out_shape=out_shapes, in_specs=[pl.BlockSpec(memor...]
    unnamed x48 -> x8, local copies, waits for them, and re-layouts: 3.24 us -> 0.02 us
    concatenate x3 -> x0, other arithmetic: 2.89 us -> none  [the longest x2 1.94 us: adjoint_rows(): jnp.concatenate([jnp.where(north_pole, flipped[2:3], flipped[0:1]), flipp...]
    ppermute x4, waiting for transfers between devices: 2.01 us -> 4.06 us  [swap(): return lax.ppermute(x, LON + LAT, pairs)]
  transfers between devices with their start and end apart: 9 -> 7, of which waited for: 6 -> 5; matrix products, arithmetic and copies ran while one was open for 11% -> 1% of each run, Pallas kernels for 0% -> 2%
where the time goes in v3:
time: 111 us; the launch traced here: 110 us
  starting transfers between devices  48.8 us (44%)
  blocking collectives  34.7 us (31%)
  waiting for transfers between devices  15.6 us (14%)
  Pallas kernels  5.41 us (5%)
  other arithmetic  3.37 us (3%)
  local copies, waits for them, and re-layouts  1.3 us (1%)
    all_to_all x2, blocking collectives, exchange(): return lax.all_to_all(v, axes, 0, 0, tiled=True)  34.7 us
    ppermute x4, starting transfers between devices, swap(): return lax.ppermute(x, LON + LAT, pairs)  25.5 us
    ppermute x2, starting transfers between devices, other_core(): return lax.ppermute(v, 'core', [(0, 1), (1, 0)])  16.9 us
    all_to_all x1, waiting for transfers between devices, exchange(): return lax.all_to_all(v, axes, 0, 0, tiled=True)  8.73 us
    all_to_all x1, starting transfers between devices, exchange(): return lax.all_to_all(v, axes, 0, 0, tiled=True)  6.41 us
    pallas_call x2, Pallas kernels, call(): pl.pallas_call(kernel, out_shape=out_shapes, in_specs=[pl.BlockSpec(memor...  5.41 us
    ppermute x4, waiting for transfers between devices, swap(): return lax.ppermute(x, LON + LAT, pairs)  4.06 us
    ppermute x2, waiting for transfers between devices, other_core(): return lax.ppermute(v, 'core', [(0, 1), (1, 0)])  2.77 us
  transfers between devices with their start and end apart: 7, of which 5 were waited for; matrix products, arithmetic and copies ran while one was open for 1% of the time, Pallas kernels for 2%

profile of v3, /device:TPU:1, one launch (start us, length us, event | category | flops | bytes accessed | tf_op | source)
XLA Modules:
  0.0 110.1 jit_solution(5552048917200470332)
XLA Ops:
  0.6 0.0 copy-start.2
  0.7 0.8 broadcast_select_fusion.6
  1.5 12.4 %collective-permute-start = (bf16[2,2,32,128]{3,2,1,0:T(8,128)(2,1)S(1)}, bf16[2,2,32,128]{3,2,1,0:T(8,128)(2,1)S(1)}, u32[]{:S(2)}, u32[]{:S(2)}) collective-permute-start(bf16[2,2,32,128]{3,2,1,0:T(8,128)(2,1)S(1)} %broadcast_select_fusion.7), channel_id=1, source_target_pairs={{0,1},{1,0},{2,3},{3,2},{4,5},{5,4},{6,7},{7,6},{8,9},{9,8},{10,11... | collective-permute-start | bytes 98312 | tf_op jit(solution)/shard_map/ppermute | solution.py:25
  13.9 1.9 %collective-permute-start.1 = (bf16[2,2,32,128]{3,2,1,0:T(8,128)(2,1)S(1)}, bf16[2,2,32,128]{3,2,1,0:T(8,128)(2,1)S(1)}, u32[]{:S(2)}, u32[]{:S(2)}) collective-permute-start(bf16[2,2,32,128]{3,2,1,0:T(8,128)(2,1)S(1)} %get-tuple-element.37), channel_id=1, source_target_pairs={{0,384},{1,2},{2,1},{3,4},{4,3},{5,6},{6,5},{7,8},{8,7},{9,10},{10... | collective-permute-start | bytes 98312 | tf_op jit(solution)/shard_map/ppermute | solution.py:25
  15.8 0.0 copy-done.2
  15.8 0.0 copy-start.1
  15.9 0.0 copy-start
  15.9 0.0 collective-permute-done
  15.9 3.2 %collective-permute-done.1 = bf16[2,2,32,128]{3,2,1,0:T(8,128)(2,1)S(1)} collective-permute-done((bf16[2,2,32,128]{3,2,1,0:T(8,128)(2,1)S(1)}, bf16[2,2,32,128]{3,2,1,0:T(8,128)(2,1)S(1)}, u32[]{:S(2)}, u32[]{:S(2)}) %collective-permute-start.1) | collective-permute-done | bytes 32800 | tf_op jit(solution)/shard_map/ppermute | solution.py:25
  19.2 0.0 copy-done.1
  19.2 0.0 copy-done
  19.2 1.9 %collective-permute-start.2 = (bf16[2,20,2,128]{3,2,1,0:T(2,128)(2,1)S(1)}, bf16[2,20,2,128]{3,2,1,0:T(2,128)(2,1)S(1)}, u32[]{:S(2)}, u32[]{:S(2)}) collective-permute-start(bf16[2,20,2,128]{3,2,1,0:T(2,128)(2,1)S(1)} %bitcast.34), channel_id=1, source_target_pairs={{0,24},{1,25},{2,26},{3,27},{4,28},{5,29},{6,30},{7,31},{8,32},{9,... | collective-permute-start | bytes 61448 | tf_op jit(solution)/shard_map/ppermute | solution.py:25
  21.2 9.3 %collective-permute-start.3 = (bf16[2,20,2,128]{3,2,1,0:T(2,128)(2,1)S(1)}, bf16[2,20,2,128]{3,2,1,0:T(2,128)(2,1)S(1)}, u32[]{:S(2)}, u32[]{:S(2)}) collective-permute-start(bf16[2,20,2,128]{3,2,1,0:T(2,128)(2,1)S(1)} %get-tuple-element.34), channel_id=1, source_target_pairs={{0,744},{1,745},{2,746},{3,747},{4,748},{5,749},{6,750},{7,751},{8... | collective-permute-start | bytes 61448 | tf_op jit(solution)/shard_map/ppermute | solution.py:25
  30.4 0.1 add_convert_fusion.1.flags
  30.5 0.2 copy.10
  30.7 0.0 collective-permute-done.2
  30.8 0.9 collective-permute-done.3
  31.7 3.3 %shard_map.75 = (bf16[2,18,48,128]{3,2,1,0:T(8,128)(2,1)S(1)}, f32[1280,128]{1,0:T(8,128)S(1)}, f32[1280,128]{1,0:T(8,128)S(1)}) custom-call(s32[4]{0:T(128)S(1)} %add_convert_fusion.1.flags, bf16[16,32,128]{2,1,0:T(8,128)(2,1)S(1)} %copy-done, bf16[16,32,128]{2,1,0:T(8,128)(2,1)S(1)} %copy-done.1, bf16[2,2,32,128]{3,2,1,0:T(8,128)(2,1)S(1)} %get-tuple-element.43.above, ...), custom_call_target="tpu_custom_call" | custom-call | flops 603979776 | bytes 2752528 | tf_op jit(solution)/shard_map/pallas_call | solution.py:175
  35.0 10.1 %collective-permute-start.4 = (f32[1280,128]{1,0:T(8,128)S(1)}, f32[1280,128]{1,0:T(8,128)}, u32[]{:S(2)}, u32[]{:S(2)}) collective-permute-start(f32[1280,128]{1,0:T(8,128)S(1)} %get-tuple-element.20), channel_id=1, source_target_pairs={{0,1},{1,0},{2,3},{3,2},{4,5},{5,4},{6,7},{7,6},{8,9},{9,8},{10,11... | collective-permute-start | bytes 1966088 | tf_op jit(solution)/shard_map/ppermute | solution.py:202
  45.2 0.2 copy.11
  45.4 1.6 %collective-permute-done.4 = f32[1280,128]{1,0:T(8,128)} collective-permute-done((f32[1280,128]{1,0:T(8,128)S(1)}, f32[1280,128]{1,0:T(8,128)}, u32[]{:S(2)}, u32[]{:S(2)}) %collective-permute-start.4) | collective-permute-done | bytes 655392 | tf_op jit(solution)/shard_map/ppermute | solution.py:202
  47.0 1.2 %add_convert_fusion = bf16[1280,128]{1,0:T(8,128)(2,1)S(1)} fusion(f32[1280,128]{1,0:T(8,128)S(1)} %get-tuple-element.19, f32[1280,128]{1,0:T(8,128)} %collective-permute-done.4), kind=kLoop, calls=%fused_computation.1 | loop fusion | flops 327680 | bytes 1638400 | tf_op jit(solution)/shard_map/convert_element_type | solution.py:205
  48.1 15.8 %all_to_all.15 = bf16[32,40,128]{2,1,0:T(8,128)(2,1)S(1)} all-to-all(bf16[32,40,128]{2,1,0:T(8,128)(2,1)S(1)} %bitcast.28), channel_id=1, replica_groups=mesh['zh'=4,'y'=8,'x'=4,'zl'=3,'core'=2] {'y','x'}, dimensions={0} | all-to-all | bytes 655360 | tf_op jit(solution)/shard_map/all_to_all | solution.py:196
  64.0 0.1 convert_reduce_fusion
  64.1 18.9 %all_to_all.16 = f32[12,40,128]{2,1,0:T(8,128)S(1)} all-to-all(f32[12,40,128]{2,1,0:T(8,128)S(1)} %broadcast_in_dim.4), channel_id=1, replica_groups=mesh['zh'=4,'y'=8,'x'=4,'zl'=3,'core'=2] {'zh','zl'}, dimensions={0} | all-to-all | bytes 491520 | tf_op jit(solution)/shard_map/all_to_all | solution.py:196
  83.0 0.8 broadcast_in_dim.5
  83.7 6.4 %all-to-all-start.2 = ((bf16[32,40,128]{2,1,0:T(8,128)(2,1)}), bf16[32,40,128]{2,1,0:T(8,128)(2,1)S(1)}, u32[]{:S(2)}, u32[]{:S(2)}) async-start(bf16[32,40,128]{2,1,0:T(8,128)(2,1)} %broadcast_in_dim.5), calls=%async_computation.2 | async-start | bytes 655360 | tf_op jit(solution)/shard_map/all_to_all | solution.py:196
  90.2 2.1 %shard_map.76 = (bf16[16,32,128]{2,1,0:T(8,128)(2,1)}, bf16[16,32,128]{2,1,0:T(8,128)(2,1)}) custom-call(s32[4]{0:T(128)S(1)} %add_convert_fusion.1.flags, bf16[2,18,48,128]{3,2,1,0:T(8,128)(2,1)S(1)} %get-tuple-element.24.ring, bf16[16,32,128]{2,1,0:T(8,128)(2,1)S(1)} %copy-done, bf16[16,32,128]{2,1,0:T(8,128)(2,1)S(1)} %copy-done.1, ...), custom_call_target="tpu_custom_call" | custom-call | flops 301989888 | bytes 1556496 | tf_op jit(solution)/shard_map/pallas_call | solution.py:175
  92.2 8.7 %all-to-all-done.2 = bf16[32,40,128]{2,1,0:T(8,128)(2,1)S(1)} async-done(((bf16[32,40,128]{2,1,0:T(8,128)(2,1)}), bf16[32,40,128]{2,1,0:T(8,128)(2,1)S(1)}, u32[]{:S(2)}, u32[]{:S(2)}) %all-to-all-start.2) | async-done | bytes 327712 | tf_op jit(solution)/shard_map/all_to_all | solution.py:196
  101.0 6.8 %collective-permute-start.5 = (bf16[1152,128]{1,0:T(8,128)(2,1)S(1)}, bf16[1152,128]{1,0:T(8,128)(2,1)S(1)}, u32[]{:S(2)}, u32[]{:S(2)}) collective-permute-start(bf16[1152,128]{1,0:T(8,128)(2,1)S(1)} %slice.20), channel_id=1, source_target_pairs={{0,1},{1,0},{2,3},{3,2},{4,5},{5,4},{6,7},{7,6},{8,9},{9,8},{10,11... | collective-permute-start | bytes 884744 | tf_op jit(solution)/shard_map/ppermute | solution.py:202
  107.8 1.2 %collective-permute-done.5 = bf16[1152,128]{1,0:T(8,128)(2,1)S(1)} collective-permute-done((bf16[1152,128]{1,0:T(8,128)(2,1)S(1)}, bf16[1152,128]{1,0:T(8,128)(2,1)S(1)}, u32[]{:S(2)}, u32[]{:S(2)}) %collective-permute-start.5) | collective-permute-done | bytes 294944 | tf_op jit(solution)/shard_map/ppermute | solution.py:202
  109.0 1.1 %convert_multiply_fusion = (f32[1152,128]{1,0:T(8,128)}, f32[1152,128]{1,0:T(8,128)}) fusion(bf16[1152,128]{1,0:T(8,128)(2,1)S(1)} %collective-permute-done.5, bf16[1152,128]{1,0:T(8,128)(2,1)S(1)} %slice.20, pred[]{:T(512)} %eq.20), kind=kLoop, calls=%fused_computation.2 | loop fusion | flops 884736 | bytes 1769473 | tf_op jit(solution)/shard_map/mul | solution.py:268
  (12 shorter events, 0.2 us)
Async XLA Ops:
  0.6 15.2 %copy-start.2 = (bf16[3,3,128,128]{3,2,1,0:T(8,128)(2,1)S(1)}, bf16[3,3,128,128]{3,2,1,0:T(8,128)(2,1)}, u32[]{:S(2)}) copy-start(bf16[3,3,128,128]{3,2,1,0:T(8,128)(2,1)} %param.7) | copy-start | bytes 884740
  1.5 14.4 %collective-permute-start = (bf16[2,2,32,128]{3,2,1,0:T(8,128)(2,1)S(1)}, bf16[2,2,32,128]{3,2,1,0:T(8,128)(2,1)S(1)}, u32[]{:S(2)}, u32[]{:S(2)}) collective-permute-start(bf16[2,2,32,128]{3,2,1,0:T(8,128)(2,1)S(1)} %broadcast_select_fusion.7), channel_id=1, source_target_pairs={{0,1},{1,0},{2,3},{3,2},{4,5},{5,4},{6,7},{7,6},{8,9},{9,8},{10,11... | collective-permute-start | bytes 98312 | tf_op jit(solution)/shard_map/ppermute | solution.py:25
  13.9 5.2 %collective-permute-start.1 = (bf16[2,2,32,128]{3,2,1,0:T(8,128)(2,1)S(1)}, bf16[2,2,32,128]{3,2,1,0:T(8,128)(2,1)S(1)}, u32[]{:S(2)}, u32[]{:S(2)}) collective-permute-start(bf16[2,2,32,128]{3,2,1,0:T(8,128)(2,1)S(1)} %get-tuple-element.37), channel_id=1, source_target_pairs={{0,384},{1,2},{2,1},{3,4},{4,3},{5,6},{6,5},{7,8},{8,7},{9,10},{10... | collective-permute-start | bytes 98312 | tf_op jit(solution)/shard_map/ppermute | solution.py:25
  15.8 3.3 %copy-start.1 = (bf16[16,32,128]{2,1,0:T(8,128)(2,1)S(1)}, bf16[16,32,128]{2,1,0:T(8,128)(2,1)}, u32[]{:S(2)}) copy-start(bf16[16,32,128]{2,1,0:T(8,128)(2,1)} %cotangent.2) | copy-start | bytes 393220
  15.9 3.3 %copy-start = (bf16[16,32,128]{2,1,0:T(8,128)(2,1)S(1)}, bf16[16,32,128]{2,1,0:T(8,128)(2,1)}, u32[]{:S(2)}) copy-start(bf16[16,32,128]{2,1,0:T(8,128)(2,1)} %fields.2) | copy-start | bytes 393220
  19.2 11.5 %collective-permute-start.2 = (bf16[2,20,2,128]{3,2,1,0:T(2,128)(2,1)S(1)}, bf16[2,20,2,128]{3,2,1,0:T(2,128)(2,1)S(1)}, u32[]{:S(2)}, u32[]{:S(2)}) collective-permute-start(bf16[2,20,2,128]{3,2,1,0:T(2,128)(2,1)S(1)} %bitcast.34), channel_id=1, source_target_pairs={{0,24},{1,25},{2,26},{3,27},{4,28},{5,29},{6,30},{7,31},{8,32},{9,... | collective-permute-start | bytes 61448 | tf_op jit(solution)/shard_map/ppermute | solution.py:25
  21.2 10.4 %collective-permute-start.3 = (bf16[2,20,2,128]{3,2,1,0:T(2,128)(2,1)S(1)}, bf16[2,20,2,128]{3,2,1,0:T(2,128)(2,1)S(1)}, u32[]{:S(2)}, u32[]{:S(2)}) collective-permute-start(bf16[2,20,2,128]{3,2,1,0:T(2,128)(2,1)S(1)} %get-tuple-element.34), channel_id=1, source_target_pairs={{0,744},{1,745},{2,746},{3,747},{4,748},{5,749},{6,750},{7,751},{8... | collective-permute-start | bytes 61448 | tf_op jit(solution)/shard_map/ppermute | solution.py:25
  30.5 1.1 %copy-start.3 = (bf16[3,3,128,128]{3,2,1,0:T(8,128)(2,1)S(1)}, bf16[3,3,128,128]{3,2,1,0:T(8,128)(2,1)}, u32[]{:S(2)}) copy-start(bf16[3,3,128,128]{3,2,1,0:T(8,128)(2,1)} %param.6) | copy-start | bytes 884740
  35.0 12.0 %collective-permute-start.4 = (f32[1280,128]{1,0:T(8,128)S(1)}, f32[1280,128]{1,0:T(8,128)}, u32[]{:S(2)}, u32[]{:S(2)}) collective-permute-start(f32[1280,128]{1,0:T(8,128)S(1)} %get-tuple-element.20), channel_id=1, source_target_pairs={{0,1},{1,0},{2,3},{3,2},{4,5},{5,4},{6,7},{7,6},{8,9},{9,8},{10,11... | collective-permute-start | bytes 1966088 | tf_op jit(solution)/shard_map/ppermute | solution.py:202
  83.7 17.2 %all-to-all-start.2 = ((bf16[32,40,128]{2,1,0:T(8,128)(2,1)}), bf16[32,40,128]{2,1,0:T(8,128)(2,1)S(1)}, u32[]{:S(2)}, u32[]{:S(2)}) async-start(bf16[32,40,128]{2,1,0:T(8,128)(2,1)} %broadcast_in_dim.5), calls=%async_computation.2 | async-start | bytes 655360 | tf_op jit(solution)/shard_map/all_to_all | solution.py:196
  101.0 8.0 %collective-permute-start.5 = (bf16[1152,128]{1,0:T(8,128)(2,1)S(1)}, bf16[1152,128]{1,0:T(8,128)(2,1)S(1)}, u32[]{:S(2)}, u32[]{:S(2)}) collective-permute-start(bf16[1152,128]{1,0:T(8,128)(2,1)S(1)} %slice.20), channel_id=1, source_target_pairs={{0,1},{1,0},{2,3},{3,2},{4,5},{5,4},{6,7},{7,6},{8,9},{9,8},{10,11... | collective-permute-start | bytes 884744 | tf_op jit(solution)/shard_map/ppermute | solution.py:202

commit v4 on v3

--- a/solution.py
+++ b/solution.py
@@ -124,10 +124,6 @@
         ].astype(jnp.bfloat16)
     own_back = gates[1, 1 : 1 + rows, 1 : 1 + cols].astype(jnp.bfloat16).reshape(-1, channels)
     own_cotangent = cotangent[...].reshape(-1, channels)
-    spare = kept.shape[0] - 9 * channels
-    if spare:
-        kept[9 * channels :] = jnp.zeros((spare, channels), jnp.float32)
-        given[9 * channels :] = jnp.zeros((spare, channels), jnp.float32)
     for tap_row in range(3):
         grad_first = outer_rows(field_taps, tap_row, rows, own_back)
         grad_second = outer_rows(hidden_taps, tap_row, rows, own_cotangent)
@@ -198,6 +194,9 @@
     def to_all(v, axes):
         return exchange(jnp.broadcast_to(v[None], (lax.axis_size(axes),) + v.shape), axes)
 
+    def total(v):
+        return jnp.sum(v.astype(jnp.float32), axis=0).astype(jnp.bfloat16)
+
     def other_core(v):
         return lax.ppermute(v, "core", [(0, 1), (1, 0)])
 
@@ -205,10 +204,10 @@
     piece = (kept + other_core(given)).astype(jnp.bfloat16)
     piece, operands = lax.optimization_barrier((piece, operands))
     outputs = finish(*operands)
-    piece = piece.reshape(lax.axis_size(SCATTER), -1, channels)
-    piece = jnp.sum(exchange(piece, SCATTER).astype(jnp.float32), axis=0)
-    piece = jnp.sum(to_all(piece, EXCHANGE), axis=0).astype(jnp.bfloat16)
-    half = to_all(piece, SCATTER).reshape(-1, channels)[: 9 * channels]
+    piece = piece.reshape(lax.axis_size(SCATTER), -1, 4, channels)
+    piece = total(exchange(piece, SCATTER))
+    piece = total(to_all(piece, EXCHANGE))
+    half = to_all(piece, SCATTER).reshape(-1, channels)
     half, outputs = lax.optimization_barrier((half, outputs))
     return half, other_core(half), outputs
 
@@ -224,8 +223,7 @@
     wide = -(-(cols + 2) // 16) * 16
     taps = 3 * channels
     flops = 2 * rows * cols * channels * channels * 9
-    split = 8 * lax.axis_size(SCATTER)
-    half = jax.ShapeDtypeStruct((-(-9 * channels // split) * split, channels), jnp.float32)
+    half = jax.ShapeDtypeStruct((9 * channels, channels), jnp.float32)
     bf16, f32 = jnp.bfloat16, jnp.float32
     ring, kept, given = call(
         ring_kernel,

time: 111 us -> 105 us (0.946)
  starting transfers between devices: 48.8 us -> 46.6 us
  blocking collectives: 34.7 us -> 32.9 us
    all_to_all x1, starting transfers between devices: 6.41 us -> 4.48 us  [exchange(): return lax.all_to_all(v, axes, 0, 0, tiled=True)]
    all_to_all x2, blocking collectives: 34.7 us -> 32.9 us  [exchange(): return lax.all_to_all(v, axes, 0, 0, tiled=True)]
where the time goes in v4:
time: 105 us
  starting transfers between devices  46.6 us (44%)
  blocking collectives  32.9 us (31%)
  waiting for transfers between devices  15.2 us (14%)
  Pallas kernels  5.41 us (5%)
  other arithmetic  2.43 us (2%)
  local copies, waits for them, and re-layouts  1.33 us (1%)
    all_to_all x2, blocking collectives, exchange(): return lax.all_to_all(v, axes, 0, 0, tiled=True)  32.9 us
    ppermute x4, starting transfers between devices, swap(): return lax.ppermute(x, LON + LAT, pairs)  25.5 us
    ppermute x2, starting transfers between devices, other_core(): return lax.ppermute(v, 'core', [(0, 1), (1, 0)])  16.6 us
    all_to_all x1, waiting for transfers between devices, exchange(): return lax.all_to_all(v, axes, 0, 0, tiled=True)  8.59 us
    pallas_call x2, Pallas kernels, call(): pl.pallas_call(kernel, out_shape=out_shapes, in_specs=[pl.BlockSpec(memor...  5.41 us
    all_to_all x1, starting transfers between devices, exchange(): return lax.all_to_all(v, axes, 0, 0, tiled=True)  4.48 us
    ppermute x4, waiting for transfers between devices, swap(): return lax.ppermute(x, LON + LAT, pairs)  4.06 us
    ppermute x2, waiting for transfers between devices, other_core(): return lax.ppermute(v, 'core', [(0, 1), (1, 0)])  2.55 us
  transfers between devices with their start and end apart: 7, of which 5 were waited for; matrix products, arithmetic and copies ran while one was open for 1% of the time, Pallas kernels for 2%

profile of v4, /device:TPU:1, one launch (start us, length us, event | category | flops | bytes accessed | tf_op | source)
XLA Modules:
  0.0 104.7 jit_solution(3507478396701961499)
XLA Ops:
  0.6 0.0 copy-start.2
  0.7 0.8 broadcast_select_fusion.6
  1.5 12.4 %collective-permute-start = (bf16[2,2,32,128]{3,2,1,0:T(8,128)(2,1)S(1)}, bf16[2,2,32,128]{3,2,1,0:T(8,128)(2,1)S(1)}, u32[]{:S(2)}, u32[]{:S(2)}) collective-permute-start(bf16[2,2,32,128]{3,2,1,0:T(8,128)(2,1)S(1)} %broadcast_select_fusion.7), channel_id=1, source_target_pairs={{0,1},{1,0},{2,3},{3,2},{4,5},{5,4},{6,7},{7,6},{8,9},{9,8},{10,11... | collective-permute-start | bytes 98312 | tf_op jit(solution)/shard_map/ppermute | solution.py:25
  13.9 1.9 %collective-permute-start.1 = (bf16[2,2,32,128]{3,2,1,0:T(8,128)(2,1)S(1)}, bf16[2,2,32,128]{3,2,1,0:T(8,128)(2,1)S(1)}, u32[]{:S(2)}, u32[]{:S(2)}) collective-permute-start(bf16[2,2,32,128]{3,2,1,0:T(8,128)(2,1)S(1)} %get-tuple-element.37), channel_id=1, source_target_pairs={{0,384},{1,2},{2,1},{3,4},{4,3},{5,6},{6,5},{7,8},{8,7},{9,10},{10... | collective-permute-start | bytes 98312 | tf_op jit(solution)/shard_map/ppermute | solution.py:25
  15.8 0.0 copy-done.2
  15.8 0.0 copy-start.1
  15.9 0.0 copy-start
  15.9 0.0 collective-permute-done
  15.9 3.2 %collective-permute-done.1 = bf16[2,2,32,128]{3,2,1,0:T(8,128)(2,1)S(1)} collective-permute-done((bf16[2,2,32,128]{3,2,1,0:T(8,128)(2,1)S(1)}, bf16[2,2,32,128]{3,2,1,0:T(8,128)(2,1)S(1)}, u32[]{:S(2)}, u32[]{:S(2)}) %collective-permute-start.1) | collective-permute-done | bytes 32800 | tf_op jit(solution)/shard_map/ppermute | solution.py:25
  19.2 0.0 copy-done.1
  19.2 1.9 %collective-permute-start.2 = (bf16[2,20,2,128]{3,2,1,0:T(2,128)(2,1)S(1)}, bf16[2,20,2,128]{3,2,1,0:T(2,128)(2,1)S(1)}, u32[]{:S(2)}, u32[]{:S(2)}) collective-permute-start(bf16[2,20,2,128]{3,2,1,0:T(2,128)(2,1)S(1)} %bitcast.35), channel_id=1, source_target_pairs={{0,24},{1,25},{2,26},{3,27},{4,28},{5,29},{6,30},{7,31},{8,32},{9,... | collective-permute-start | bytes 61448 | tf_op jit(solution)/shard_map/ppermute | solution.py:25
  21.2 9.3 %collective-permute-start.3 = (bf16[2,20,2,128]{3,2,1,0:T(2,128)(2,1)S(1)}, bf16[2,20,2,128]{3,2,1,0:T(2,128)(2,1)S(1)}, u32[]{:S(2)}, u32[]{:S(2)}) collective-permute-start(bf16[2,20,2,128]{3,2,1,0:T(2,128)(2,1)S(1)} %get-tuple-element.34), channel_id=1, source_target_pairs={{0,744},{1,745},{2,746},{3,747},{4,748},{5,749},{6,750},{7,751},{8... | collective-permute-start | bytes 61448 | tf_op jit(solution)/shard_map/ppermute | solution.py:25
  30.4 0.1 add_convert_fusion.1.flags
  30.5 0.2 copy.10
  30.7 0.0 collective-permute-done.2
  30.8 0.9 collective-permute-done.3
  31.7 3.3 %shard_map.75 = (bf16[2,18,48,128]{3,2,1,0:T(8,128)(2,1)S(1)}, f32[1152,128]{1,0:T(8,128)S(1)}, f32[1152,128]{1,0:T(8,128)S(1)}) custom-call(s32[4]{0:T(128)S(1)} %add_convert_fusion.1.flags, bf16[16,32,128]{2,1,0:T(8,128)(2,1)S(1)} %copy-done, bf16[16,32,128]{2,1,0:T(8,128)(2,1)S(1)} %copy-done.1, bf16[2,2,32,128]{3,2,1,0:T(8,128)(2,1)S(1)} %get-tuple-element.43.above, ...), custom_call_target="tpu_custom_call" | custom-call | flops 603979776 | bytes 2621456 | tf_op jit(solution)/shard_map/pallas_call | solution.py:171
  35.0 10.1 %collective-permute-start.4 = (f32[1152,128]{1,0:T(8,128)S(1)}, f32[1152,128]{1,0:T(8,128)S(1)}, u32[]{:S(2)}, u32[]{:S(2)}) collective-permute-start(f32[1152,128]{1,0:T(8,128)S(1)} %get-tuple-element.20), channel_id=1, source_target_pairs={{0,1},{1,0},{2,3},{3,2},{4,5},{5,4},{6,7},{7,6},{8,9},{9,8},{10,11... | collective-permute-start | bytes 1769480 | tf_op jit(solution)/shard_map/ppermute | solution.py:201
  45.2 0.2 copy.11
  45.4 1.4 %collective-permute-done.4 = f32[1152,128]{1,0:T(8,128)S(1)} collective-permute-done((f32[1152,128]{1,0:T(8,128)S(1)}, f32[1152,128]{1,0:T(8,128)S(1)}, u32[]{:S(2)}, u32[]{:S(2)}) %collective-permute-start.4) | collective-permute-done | bytes 589856 | tf_op jit(solution)/shard_map/ppermute | solution.py:201
  46.8 0.1 add_convert_fusion
  46.8 15.3 %all_to_all.15 = bf16[32,9,4,128]{3,2,1,0:T(4,128)(2,1)S(1)} all-to-all(bf16[32,9,4,128]{3,2,1,0:T(4,128)(2,1)S(1)} %bitcast.30), channel_id=1, replica_groups=mesh['zh'=4,'y'=8,'x'=4,'zl'=3,'core'=2] {'y','x'}, dimensions={0} | all-to-all | bytes 589824 | tf_op jit(solution)/shard_map/all_to_all | solution.py:192
  62.2 0.1 reduce_sum.24
  62.3 17.5 %all_to_all.16 = bf16[12,9,4,128]{3,2,1,0:T(4,128)(2,1)S(1)} all-to-all(bf16[12,9,4,128]{3,2,1,0:T(4,128)(2,1)S(1)} %broadcast_in_dim.4), channel_id=1, replica_groups=mesh['zh'=4,'y'=8,'x'=4,'zl'=3,'core'=2] {'zh','zl'}, dimensions={0} | all-to-all | bytes 221184 | tf_op jit(solution)/shard_map/all_to_all | solution.py:192
  79.9 0.1 reduce_sum.25
  79.9 0.8 broadcast_in_dim.5
  80.7 4.5 %all-to-all-start.2 = ((bf16[32,9,4,128]{3,2,1,0:T(4,128)(2,1)}), bf16[32,9,4,128]{3,2,1,0:T(4,128)(2,1)S(1)}, u32[]{:S(2)}, u32[]{:S(2)}) async-start(bf16[32,9,4,128]{3,2,1,0:T(4,128)(2,1)} %broadcast_in_dim.5), calls=%async_computation.2 | async-start | bytes 589824 | tf_op jit(solution)/shard_map/all_to_all | solution.py:192
  85.2 2.1 %shard_map.76 = (bf16[16,32,128]{2,1,0:T(8,128)(2,1)}, bf16[16,32,128]{2,1,0:T(8,128)(2,1)}) custom-call(s32[4]{0:T(128)S(1)} %add_convert_fusion.1.flags, bf16[2,18,48,128]{3,2,1,0:T(8,128)(2,1)S(1)} %get-tuple-element.24.ring, bf16[16,32,128]{2,1,0:T(8,128)(2,1)S(1)} %copy-done, bf16[16,32,128]{2,1,0:T(8,128)(2,1)S(1)} %copy-done.1, ...), custom_call_target="tpu_custom_call" | custom-call | flops 301989888 | bytes 1556496 | tf_op jit(solution)/shard_map/pallas_call | solution.py:171
  87.3 8.6 %all-to-all-done.2 = bf16[32,9,4,128]{3,2,1,0:T(4,128)(2,1)S(1)} async-done(((bf16[32,9,4,128]{3,2,1,0:T(4,128)(2,1)}), bf16[32,9,4,128]{3,2,1,0:T(4,128)(2,1)S(1)}, u32[]{:S(2)}, u32[]{:S(2)}) %all-to-all-start.2) | async-done | bytes 294944 | tf_op jit(solution)/shard_map/all_to_all | solution.py:192
  95.9 6.5 %collective-permute-start.5 = (bf16[1152,128]{1,0:T(8,128)(2,1)S(1)}, bf16[1152,128]{1,0:T(8,128)(2,1)S(1)}, u32[]{:S(2)}, u32[]{:S(2)}) collective-permute-start(bf16[1152,128]{1,0:T(8,128)(2,1)S(1)} %bitcast.28), channel_id=1, source_target_pairs={{0,1},{1,0},{2,3},{3,2},{4,5},{5,4},{6,7},{7,6},{8,9},{9,8},{10,11... | collective-permute-start | bytes 884744 | tf_op jit(solution)/shard_map/ppermute | solution.py:201
  102.4 1.2 %collective-permute-done.5 = bf16[1152,128]{1,0:T(8,128)(2,1)S(1)} collective-permute-done((bf16[1152,128]{1,0:T(8,128)(2,1)S(1)}, bf16[1152,128]{1,0:T(8,128)(2,1)S(1)}, u32[]{:S(2)}, u32[]{:S(2)}) %collective-permute-start.5) | collective-permute-done | bytes 294944 | tf_op jit(solution)/shard_map/ppermute | solution.py:201
  103.6 1.1 %convert_multiply_fusion = (f32[1152,128]{1,0:T(8,128)}, f32[1152,128]{1,0:T(8,128)}) fusion(bf16[1152,128]{1,0:T(8,128)(2,1)S(1)} %collective-permute-done.5, bf16[1152,128]{1,0:T(8,128)(2,1)S(1)} %bitcast.29, pred[]{:T(512)} %eq.20), kind=kLoop, calls=%fused_computation | loop fusion | flops 884736 | bytes 1769473 | tf_op jit(solution)/shard_map/mul | solution.py:266
  (11 shorter events, 0.2 us)
Async XLA Ops:
  0.6 15.2 %copy-start.2 = (bf16[3,3,128,128]{3,2,1,0:T(8,128)(2,1)S(1)}, bf16[3,3,128,128]{3,2,1,0:T(8,128)(2,1)}, u32[]{:S(2)}) copy-start(bf16[3,3,128,128]{3,2,1,0:T(8,128)(2,1)} %param.7) | copy-start | bytes 884740
  1.5 14.4 %collective-permute-start = (bf16[2,2,32,128]{3,2,1,0:T(8,128)(2,1)S(1)}, bf16[2,2,32,128]{3,2,1,0:T(8,128)(2,1)S(1)}, u32[]{:S(2)}, u32[]{:S(2)}) collective-permute-start(bf16[2,2,32,128]{3,2,1,0:T(8,128)(2,1)S(1)} %broadcast_select_fusion.7), channel_id=1, source_target_pairs={{0,1},{1,0},{2,3},{3,2},{4,5},{5,4},{6,7},{7,6},{8,9},{9,8},{10,11... | collective-permute-start | bytes 98312 | tf_op jit(solution)/shard_map/ppermute | solution.py:25
  13.9 5.2 %collective-permute-start.1 = (bf16[2,2,32,128]{3,2,1,0:T(8,128)(2,1)S(1)}, bf16[2,2,32,128]{3,2,1,0:T(8,128)(2,1)S(1)}, u32[]{:S(2)}, u32[]{:S(2)}) collective-permute-start(bf16[2,2,32,128]{3,2,1,0:T(8,128)(2,1)S(1)} %get-tuple-element.37), channel_id=1, source_target_pairs={{0,384},{1,2},{2,1},{3,4},{4,3},{5,6},{6,5},{7,8},{8,7},{9,10},{10... | collective-permute-start | bytes 98312 | tf_op jit(solution)/shard_map/ppermute | solution.py:25
  15.8 3.3 %copy-start.1 = (bf16[16,32,128]{2,1,0:T(8,128)(2,1)S(1)}, bf16[16,32,128]{2,1,0:T(8,128)(2,1)}, u32[]{:S(2)}) copy-start(bf16[16,32,128]{2,1,0:T(8,128)(2,1)} %cotangent.2) | copy-start | bytes 393220
  15.9 3.3 %copy-start = (bf16[16,32,128]{2,1,0:T(8,128)(2,1)S(1)}, bf16[16,32,128]{2,1,0:T(8,128)(2,1)}, u32[]{:S(2)}) copy-start(bf16[16,32,128]{2,1,0:T(8,128)(2,1)} %fields.2) | copy-start | bytes 393220
  19.2 11.5 %collective-permute-start.2 = (bf16[2,20,2,128]{3,2,1,0:T(2,128)(2,1)S(1)}, bf16[2,20,2,128]{3,2,1,0:T(2,128)(2,1)S(1)}, u32[]{:S(2)}, u32[]{:S(2)}) collective-permute-start(bf16[2,20,2,128]{3,2,1,0:T(2,128)(2,1)S(1)} %bitcast.35), channel_id=1, source_target_pairs={{0,24},{1,25},{2,26},{3,27},{4,28},{5,29},{6,30},{7,31},{8,32},{9,... | collective-permute-start | bytes 61448 | tf_op jit(solution)/shard_map/ppermute | solution.py:25
  21.2 10.4 %collective-permute-start.3 = (bf16[2,20,2,128]{3,2,1,0:T(2,128)(2,1)S(1)}, bf16[2,20,2,128]{3,2,1,0:T(2,128)(2,1)S(1)}, u32[]{:S(2)}, u32[]{:S(2)}) collective-permute-start(bf16[2,20,2,128]{3,2,1,0:T(2,128)(2,1)S(1)} %get-tuple-element.34), channel_id=1, source_target_pairs={{0,744},{1,745},{2,746},{3,747},{4,748},{5,749},{6,750},{7,751},{8... | collective-permute-start | bytes 61448 | tf_op jit(solution)/shard_map/ppermute | solution.py:25
  30.5 1.1 %copy-start.3 = (bf16[3,3,128,128]{3,2,1,0:T(8,128)(2,1)S(1)}, bf16[3,3,128,128]{3,2,1,0:T(8,128)(2,1)}, u32[]{:S(2)}) copy-start(bf16[3,3,128,128]{3,2,1,0:T(8,128)(2,1)} %param.6) | copy-start | bytes 884740
  35.0 11.8 %collective-permute-start.4 = (f32[1152,128]{1,0:T(8,128)S(1)}, f32[1152,128]{1,0:T(8,128)S(1)}, u32[]{:S(2)}, u32[]{:S(2)}) collective-permute-start(f32[1152,128]{1,0:T(8,128)S(1)} %get-tuple-element.20), channel_id=1, source_target_pairs={{0,1},{1,0},{2,3},{3,2},{4,5},{5,4},{6,7},{7,6},{8,9},{9,8},{10,11... | collective-permute-start | bytes 1769480 | tf_op jit(solution)/shard_map/ppermute | solution.py:201
  80.7 15.2 %all-to-all-start.2 = ((bf16[32,9,4,128]{3,2,1,0:T(4,128)(2,1)}), bf16[32,9,4,128]{3,2,1,0:T(4,128)(2,1)S(1)}, u32[]{:S(2)}, u32[]{:S(2)}) async-start(bf16[32,9,4,128]{3,2,1,0:T(4,128)(2,1)} %broadcast_in_dim.5), calls=%async_computation.2 | async-start | bytes 589824 | tf_op jit(solution)/shard_map/all_to_all | solution.py:192
  95.9 7.7 %collective-permute-start.5 = (bf16[1152,128]{1,0:T(8,128)(2,1)S(1)}, bf16[1152,128]{1,0:T(8,128)(2,1)S(1)}, u32[]{:S(2)}, u32[]{:S(2)}) collective-permute-start(bf16[1152,128]{1,0:T(8,128)(2,1)S(1)} %bitcast.28), channel_id=1, source_target_pairs={{0,1},{1,0},{2,3},{3,2},{4,5},{5,4},{6,7},{7,6},{8,9},{9,8},{10,11... | collective-permute-start | bytes 884744 | tf_op jit(solution)/shard_map/ppermute | solution.py:201

commit v5 on v4

--- a/solution.py
+++ b/solution.py
@@ -63,14 +63,42 @@
     return total.reshape(count, -1, total.shape[-1])
 
 
-def outer_rows(taps_ref, tap_row, rows, upstream):
+def conv_pairs(taps_ref, pairs, weight_ref):
+    zero = jnp.zeros(weight_ref.shape[1:], weight_ref.dtype)
+    depth, channels = weight_ref.shape[0], weight_ref.shape[-1]
+    total = None
+    for start in range(0, depth + 1, 2):
+        taps = jnp.concatenate(
+            [
+                jnp.concatenate([taps_ref[2 * pair + start + step] for pair in range(pairs)], axis=0)
+                for step in range(2)
+            ],
+            axis=1,
+        )
+        weight = jnp.concatenate(
+            [
+                jnp.concatenate(
+                    [
+                        weight_ref[row - out] if 0 <= row - out < depth else zero
+                        for out in range(2)
+                    ],
+                    axis=1,
+                )
+                for row in (start, start + 1)
+            ],
+            axis=0,
+        )
+        term = jnp.dot(taps, weight, preferred_element_type=jnp.float32)
+        total = term if total is None else total + term
+    total = total.reshape(pairs, -1, 2 * channels)
+    return total[:, :, :channels], total[:, :, channels:]
+
+
+def outer_rows(taps_ref, tap_row, rows, upstream_turned):
     taps = taps_ref[tap_row : tap_row + rows]
-    return lax.dot_general(
-        taps.reshape(-1, taps.shape[-1]),
-        upstream,
-        (((0,), (0,)), ((), ())),
-        preferred_element_type=jnp.float32,
-    )
+    return jnp.dot(
+        upstream_turned, taps.reshape(-1, taps.shape[-1]), preferred_element_type=jnp.float32
+    ).T
 
 
 def ring_kernel(
@@ -97,8 +125,11 @@
             0, 1 : 3 + rows, 7 + tap : 7 + tap + cols
         ].astype(jnp.bfloat16)
     of_fields, of_cotangent = taps.at[0], taps.at[1]
-    sums[0] = conv_rows(of_fields, 0, rows + 2, first, (0, 1, 2))
-    sums[1] = conv_rows(of_cotangent, 0, rows + 2, turned_second, (0, 1, 2))
+    pairs = (rows + 2) // 2
+    for which, weight in enumerate((first, turned_second)):
+        for out, part in enumerate(conv_pairs(taps.at[which], pairs, weight)):
+            for pair in range(pairs):
+                sums[which, 2 * pair + out] = part[pair]
 
     @pl.when(north)
     def _():
@@ -122,22 +153,14 @@
         hidden_taps[:, :, channels * tap : channels * (tap + 1)] = gates[
             0, :, tap : tap + cols
         ].astype(jnp.bfloat16)
-    own_back = gates[1, 1 : 1 + rows, 1 : 1 + cols].astype(jnp.bfloat16).reshape(-1, channels)
-    own_cotangent = cotangent[...].reshape(-1, channels)
+    own_back = gates[1, 1 : 1 + rows, 1 : 1 + cols].astype(jnp.bfloat16).reshape(-1, channels).T
+    own_cotangent = cotangent[...].reshape(-1, channels).T
     for tap_row in range(3):
         grad_first = outer_rows(field_taps, tap_row, rows, own_back)
         grad_second = outer_rows(hidden_taps, tap_row, rows, own_cotangent)
         place = slice(3 * channels * tap_row, 3 * channels * (tap_row + 1))
-
-        @pl.when(low)
-        def _():
-            kept[place] = grad_first
-            given[place] = grad_second
-
-        @pl.when(jnp.logical_not(low))
-        def _():
-            kept[place] = grad_second
-            given[place] = grad_first
+        kept[place] = jnp.where(low, grad_first, grad_second)
+        given[place] = jnp.where(low, grad_second, grad_first)
 
 
 def output_kernel(flags, ring, fields, cotangent, second, turned_first, output, back_fields, wide_ring, taps, sums):
@@ -149,10 +172,14 @@
             taps[which, :, :, channels * tap : channels * (tap + 1)] = wide_ring[
                 which, :, tap : tap + cols
             ].astype(jnp.bfloat16)
-    second_sum = conv_rows(taps.at[0], 0, rows, second, (0, 1, 2))
-    output[...] = (fields[...].astype(jnp.float32) + second_sum).astype(jnp.bfloat16)
+    for out, part in enumerate(conv_pairs(taps.at[0], rows // 2, second)):
+        for pair in range(rows // 2):
+            row = 2 * pair + out
+            output[row] = (fields[row].astype(jnp.float32) + part[pair]).astype(jnp.bfloat16)
     of_back = taps.at[1]
-    sums[...] = conv_rows(of_back, 0, rows, turned_first, (0, 1, 2))
+    for out, part in enumerate(conv_pairs(of_back, rows // 2, turned_first)):
+        for pair in range(rows // 2):
+            sums[2 * pair + out] = part[pair]
 
     @pl.when(north)
     def _():
@@ -202,14 +229,12 @@
 
     channels = kept.shape[-1]
     piece = (kept + other_core(given)).astype(jnp.bfloat16)
-    piece, operands = lax.optimization_barrier((piece, operands))
-    outputs = finish(*operands)
     piece = piece.reshape(lax.axis_size(SCATTER), -1, 4, channels)
     piece = total(exchange(piece, SCATTER))
     piece = total(to_all(piece, EXCHANGE))
     half = to_all(piece, SCATTER).reshape(-1, channels)
-    half, outputs = lax.optimization_barrier((half, outputs))
-    return half, other_core(half), outputs
+    half, operands = lax.optimization_barrier((half, operands))
+    return half, other_core(half), finish(*operands)
 
 
 def per_device(fields, cotangent, weight_first, weight_second):
@@ -220,6 +245,8 @@
     low_core = lax.axis_index("core") == 0
     flags = jnp.stack([north_pole, south_pole, low_core, low_core]).astype(jnp.int32)
     edges = halo_of_two(jnp.stack([fields, cotangent]), north_pole, south_pole)
+    turned_first = by_row(turned(weight_first))
+    edges, turned_first = lax.optimization_barrier((edges, turned_first))
     wide = -(-(cols + 2) // 16) * 16
     taps = 3 * channels
     flops = 2 * rows * cols * channels * channels * 9
@@ -258,7 +285,7 @@
         kept,
         given,
         finish,
-        (flags, ring, fields, cotangent, by_row(weight_second), by_row(turned(weight_first))),
+        (flags, ring, fields, cotangent, by_row(weight_second), turned_first),
     )
     cells_total = rows * lax.axis_size(LAT) * cols * lax.axis_size(LON)
     grad_scale = 1.0 / math.sqrt(cells_total)

time: 105 us -> 104 us (level)
  blocking collectives: 32.9 us -> 47.8 us
  waiting for transfers between devices: 15.2 us -> 5.41 us
  starting transfers between devices: 46.6 us -> 42.3 us
  Pallas kernels: 5.41 us -> 4.28 us
    all_to_all x2 -> x3, blocking collectives: 32.9 us -> 47.8 us  [exchange(): return lax.all_to_all(v, axes, 0, 0, tiled=True)]
    all_to_all x1 -> x0, waiting for transfers between devices: 8.59 us -> none  [exchange(): return lax.all_to_all(v, axes, 0, 0, tiled=True)]
    all_to_all x1 -> x0, starting transfers between devices: 4.48 us -> none  [exchange(): return lax.all_to_all(v, axes, 0, 0, tiled=True)]
    pallas_call x2, Pallas kernels: 5.41 us -> 4.28 us  [call(): pl.pallas_call(kernel, out_shape=out_shapes, in_specs=[pl.BlockSpec(memor...]
  transfers between devices with their start and end apart: 7 -> 6, of which waited for: 5 -> 3; matrix products, arithmetic and copies ran while one was open for 1% -> 1% of each run, Pallas kernels for 2% -> 2%
where the time goes in v5:
time: 104 us
  blocking collectives  47.8 us (46%)
  starting transfers between devices  42.3 us (41%)
  waiting for transfers between devices  5.41 us (5%)
  Pallas kernels  4.28 us (4%)
  other arithmetic  2.4 us (2%)
    all_to_all x3, blocking collectives, exchange(): return lax.all_to_all(v, axes, 0, 0, tiled=True)  47.8 us
    ppermute x4, starting transfers between devices, swap(): return lax.ppermute(x, LON + LAT, pairs)  25.6 us
    ppermute x2, starting transfers between devices, other_core(): return lax.ppermute(v, 'core', [(0, 1), (1, 0)])  16.7 us
    pallas_call x2, Pallas kernels, call(): pl.pallas_call(kernel, out_shape=out_shapes, in_specs=[pl.BlockSpec(memor...  4.28 us
    ppermute x4, waiting for transfers between devices, swap(): return lax.ppermute(x, LON + LAT, pairs)  3.8 us
  transfers between devices with their start and end apart: 6, of which 3 were waited for; matrix products, arithmetic and copies ran while one was open for 1% of the time, Pallas kernels for 2%

profile of v5, /device:TPU:1, one launch (start us, length us, event | category | flops | bytes accessed | tf_op | source)
XLA Modules:
  0.0 103.7 jit_solution(10621918410732568569)
XLA Ops:
  0.6 0.0 copy-start.3
  0.7 0.8 broadcast_select_fusion.6
  1.5 12.4 %collective-permute-start = (bf16[2,2,32,128]{3,2,1,0:T(8,128)(2,1)S(1)}, bf16[2,2,32,128]{3,2,1,0:T(8,128)(2,1)S(1)}, u32[]{:S(2)}, u32[]{:S(2)}) collective-permute-start(bf16[2,2,32,128]{3,2,1,0:T(8,128)(2,1)S(1)} %broadcast_select_fusion.7), channel_id=1, source_target_pairs={{0,1},{1,0},{2,3},{3,2},{4,5},{5,4},{6,7},{7,6},{8,9},{9,8},{10,11... | collective-permute-start | bytes 98312 | tf_op jit(solution)/shard_map/ppermute | solution.py:25
  13.9 0.0 copy-start.2
  13.9 2.1 %collective-permute-start.1 = (bf16[2,2,32,128]{3,2,1,0:T(8,128)(2,1)S(1)}, bf16[2,2,32,128]{3,2,1,0:T(8,128)(2,1)S(1)}, u32[]{:S(2)}, u32[]{:S(2)}) collective-permute-start(bf16[2,2,32,128]{3,2,1,0:T(8,128)(2,1)S(1)} %get-tuple-element.41), channel_id=1, source_target_pairs={{0,384},{1,2},{2,1},{3,4},{4,3},{5,6},{6,5},{7,8},{8,7},{9,10},{10... | collective-permute-start | bytes 98312 | tf_op jit(solution)/shard_map/ppermute | solution.py:25
  16.0 0.0 copy-start.1
  16.1 0.0 copy-start
  16.1 0.0 collective-permute-done
  16.1 3.2 %collective-permute-done.1 = bf16[2,2,32,128]{3,2,1,0:T(8,128)(2,1)S(1)} collective-permute-done((bf16[2,2,32,128]{3,2,1,0:T(8,128)(2,1)S(1)}, bf16[2,2,32,128]{3,2,1,0:T(8,128)(2,1)S(1)}, u32[]{:S(2)}, u32[]{:S(2)}) %collective-permute-start.1) | collective-permute-done | bytes 32800 | tf_op jit(solution)/shard_map/ppermute | solution.py:25
  19.3 0.0 copy-done.1
  19.3 0.0 copy-done
  19.4 1.9 %collective-permute-start.2 = (bf16[2,20,2,128]{3,2,1,0:T(2,128)(2,1)S(1)}, bf16[2,20,2,128]{3,2,1,0:T(2,128)(2,1)S(1)}, u32[]{:S(2)}, u32[]{:S(2)}) collective-permute-start(bf16[2,20,2,128]{3,2,1,0:T(2,128)(2,1)S(1)} %bitcast.35), channel_id=1, source_target_pairs={{0,24},{1,25},{2,26},{3,27},{4,28},{5,29},{6,30},{7,31},{8,32},{9,... | collective-permute-start | bytes 61448 | tf_op jit(solution)/shard_map/ppermute | solution.py:25
  21.3 9.3 %collective-permute-start.3 = (bf16[2,20,2,128]{3,2,1,0:T(2,128)(2,1)S(1)}, bf16[2,20,2,128]{3,2,1,0:T(2,128)(2,1)S(1)}, u32[]{:S(2)}, u32[]{:S(2)}) collective-permute-start(bf16[2,20,2,128]{3,2,1,0:T(2,128)(2,1)S(1)} %get-tuple-element.38), channel_id=1, source_target_pairs={{0,744},{1,745},{2,746},{3,747},{4,748},{5,749},{6,750},{7,751},{8... | collective-permute-start | bytes 61448 | tf_op jit(solution)/shard_map/ppermute | solution.py:25
  30.6 0.1 add_convert_fusion.1.flags
  30.7 0.2 copy.10
  30.9 0.2 copy.11
  31.1 0.0 collective-permute-done.2
  31.1 0.6 collective-permute-done.3
  31.8 2.4 %shard_map.75 = (bf16[2,18,48,128]{3,2,1,0:T(8,128)(2,1)S(1)}, f32[1152,128]{1,0:T(8,128)S(1)}, f32[1152,128]{1,0:T(8,128)S(1)}) custom-call(s32[4]{0:T(128)S(1)} %add_convert_fusion.1.flags, bf16[16,32,128]{2,1,0:T(8,128)(2,1)S(1)} %copy-done, bf16[16,32,128]{2,1,0:T(8,128)(2,1)S(1)} %copy-done.1, bf16[2,2,32,128]{3,2,1,0:T(8,128)(2,1)S(1)} %get-tuple-element.21.above, ...), custom_call_target="tpu_custom_call" | custom-call | flops 603979776 | bytes 2621456 | tf_op jit(solution)/shard_map/pallas_call | solution.py:198
  34.2 10.2 %collective-permute-start.4 = (f32[1152,128]{1,0:T(8,128)S(1)}, f32[1152,128]{1,0:T(8,128)S(1)}, u32[]{:S(2)}, u32[]{:S(2)}) collective-permute-start(f32[1152,128]{1,0:T(8,128)S(1)} %get-tuple-element.26), channel_id=1, source_target_pairs={{0,1},{1,0},{2,3},{3,2},{4,5},{5,4},{6,7},{7,6},{8,9},{9,8},{10,11... | collective-permute-start | bytes 1769480 | tf_op jit(solution)/shard_map/ppermute | solution.py:228
  44.4 1.6 %collective-permute-done.4 = f32[1152,128]{1,0:T(8,128)S(1)} collective-permute-done((f32[1152,128]{1,0:T(8,128)S(1)}, f32[1152,128]{1,0:T(8,128)S(1)}, u32[]{:S(2)}, u32[]{:S(2)}) %collective-permute-start.4) | collective-permute-done | bytes 589856 | tf_op jit(solution)/shard_map/ppermute | solution.py:228
  46.0 0.1 add_convert_fusion
  46.1 15.3 %all_to_all.15 = bf16[32,9,4,128]{3,2,1,0:T(4,128)(2,1)S(1)} all-to-all(bf16[32,9,4,128]{3,2,1,0:T(4,128)(2,1)S(1)} %bitcast.30), channel_id=1, replica_groups=mesh['zh'=4,'y'=8,'x'=4,'zl'=3,'core'=2] {'y','x'}, dimensions={0} | all-to-all | bytes 589824 | tf_op jit(solution)/shard_map/all_to_all | solution.py:219
  61.4 0.1 reduce_sum.24
  61.6 17.5 %all_to_all.16 = bf16[12,9,4,128]{3,2,1,0:T(4,128)(2,1)S(1)} all-to-all(bf16[12,9,4,128]{3,2,1,0:T(4,128)(2,1)S(1)} %broadcast_in_dim.4), channel_id=1, replica_groups=mesh['zh'=4,'y'=8,'x'=4,'zl'=3,'core'=2] {'zh','zl'}, dimensions={0} | all-to-all | bytes 221184 | tf_op jit(solution)/shard_map/all_to_all | solution.py:219
  79.1 0.1 reduce_sum.25
  79.2 0.1 broadcast_in_dim.5
  79.3 15.0 %all_to_all.17 = bf16[32,9,4,128]{3,2,1,0:T(4,128)(2,1)S(1)} all-to-all(bf16[32,9,4,128]{3,2,1,0:T(4,128)(2,1)S(1)} %broadcast_in_dim.5), channel_id=1, replica_groups=mesh['zh'=4,'y'=8,'x'=4,'zl'=3,'core'=2] {'y','x'}, dimensions={0} | all-to-all | bytes 589824 | tf_op jit(solution)/shard_map/all_to_all | solution.py:219
  94.2 6.5 %collective-permute-start.5 = (bf16[1152,128]{1,0:T(8,128)(2,1)S(1)}, bf16[1152,128]{1,0:T(8,128)(2,1)S(1)}, u32[]{:S(2)}, u32[]{:S(2)}) collective-permute-start(bf16[1152,128]{1,0:T(8,128)(2,1)S(1)} %bitcast.28), channel_id=1, source_target_pairs={{0,1},{1,0},{2,3},{3,2},{4,5},{5,4},{6,7},{7,6},{8,9},{9,8},{10,11... | collective-permute-start | bytes 884744 | tf_op jit(solution)/shard_map/ppermute | solution.py:228
  100.7 1.9 %shard_map.76 = (bf16[16,32,128]{2,1,0:T(8,128)(2,1)}, bf16[16,32,128]{2,1,0:T(8,128)(2,1)}) custom-call(s32[4]{0:T(128)S(1)} %add_convert_fusion.1.flags, bf16[2,18,48,128]{3,2,1,0:T(8,128)(2,1)S(1)} %get-tuple-element.30.ring, bf16[16,32,128]{2,1,0:T(8,128)(2,1)S(1)} %copy-done, bf16[16,32,128]{2,1,0:T(8,128)(2,1)S(1)} %copy-done.1, ...), custom_call_target="tpu_custom_call" | custom-call | flops 301989888 | bytes 1556496 | tf_op jit(solution)/shard_map/pallas_call | solution.py:198
  102.6 0.0 collective-permute-done.5
  102.6 1.1 %convert_multiply_fusion = (f32[1152,128]{1,0:T(8,128)}, f32[1152,128]{1,0:T(8,128)}) fusion(bf16[1152,128]{1,0:T(8,128)(2,1)S(1)} %collective-permute-done.5, bf16[1152,128]{1,0:T(8,128)(2,1)S(1)} %bitcast.29, pred[]{:T(512)} %eq.20), kind=kLoop, calls=%fused_computation | loop fusion | flops 884736 | bytes 1769473 | tf_op jit(solution)/shard_map/mul | solution.py:293
  (10 shorter events, 0.2 us)
Async XLA Ops:
  0.6 15.3 %copy-start.3 = (bf16[3,3,128,128]{3,2,1,0:T(8,128)(2,1)S(1)}, bf16[3,3,128,128]{3,2,1,0:T(8,128)(2,1)}, u32[]{:S(2)}) copy-start(bf16[3,3,128,128]{3,2,1,0:T(8,128)(2,1)} %param.6) | copy-start | bytes 884740
  1.5 14.6 %collective-permute-start = (bf16[2,2,32,128]{3,2,1,0:T(8,128)(2,1)S(1)}, bf16[2,2,32,128]{3,2,1,0:T(8,128)(2,1)S(1)}, u32[]{:S(2)}, u32[]{:S(2)}) collective-permute-start(bf16[2,2,32,128]{3,2,1,0:T(8,128)(2,1)S(1)} %broadcast_select_fusion.7), channel_id=1, source_target_pairs={{0,1},{1,0},{2,3},{3,2},{4,5},{5,4},{6,7},{7,6},{8,9},{9,8},{10,11... | collective-permute-start | bytes 98312 | tf_op jit(solution)/shard_map/ppermute | solution.py:25
  13.9 2.1 %copy-start.2 = (bf16[3,3,128,128]{3,2,1,0:T(8,128)(2,1)S(1)}, bf16[3,3,128,128]{3,2,1,0:T(8,128)(2,1)}, u32[]{:S(2)}) copy-start(bf16[3,3,128,128]{3,2,1,0:T(8,128)(2,1)} %param.7) | copy-start | bytes 884740
  13.9 5.4 %collective-permute-start.1 = (bf16[2,2,32,128]{3,2,1,0:T(8,128)(2,1)S(1)}, bf16[2,2,32,128]{3,2,1,0:T(8,128)(2,1)S(1)}, u32[]{:S(2)}, u32[]{:S(2)}) collective-permute-start(bf16[2,2,32,128]{3,2,1,0:T(8,128)(2,1)S(1)} %get-tuple-element.41), channel_id=1, source_target_pairs={{0,384},{1,2},{2,1},{3,4},{4,3},{5,6},{6,5},{7,8},{8,7},{9,10},{10... | collective-permute-start | bytes 98312 | tf_op jit(solution)/shard_map/ppermute | solution.py:25
  16.0 3.3 %copy-start.1 = (bf16[16,32,128]{2,1,0:T(8,128)(2,1)S(1)}, bf16[16,32,128]{2,1,0:T(8,128)(2,1)}, u32[]{:S(2)}) copy-start(bf16[16,32,128]{2,1,0:T(8,128)(2,1)} %cotangent.2) | copy-start | bytes 393220
  16.1 3.2 %copy-start = (bf16[16,32,128]{2,1,0:T(8,128)(2,1)S(1)}, bf16[16,32,128]{2,1,0:T(8,128)(2,1)}, u32[]{:S(2)}) copy-start(bf16[16,32,128]{2,1,0:T(8,128)(2,1)} %fields.2) | copy-start | bytes 393220
  19.4 11.7 %collective-permute-start.2 = (bf16[2,20,2,128]{3,2,1,0:T(2,128)(2,1)S(1)}, bf16[2,20,2,128]{3,2,1,0:T(2,128)(2,1)S(1)}, u32[]{:S(2)}, u32[]{:S(2)}) collective-permute-start(bf16[2,20,2,128]{3,2,1,0:T(2,128)(2,1)S(1)} %bitcast.35), channel_id=1, source_target_pairs={{0,24},{1,25},{2,26},{3,27},{4,28},{5,29},{6,30},{7,31},{8,32},{9,... | collective-permute-start | bytes 61448 | tf_op jit(solution)/shard_map/ppermute | solution.py:25
  21.3 10.4 %collective-permute-start.3 = (bf16[2,20,2,128]{3,2,1,0:T(2,128)(2,1)S(1)}, bf16[2,20,2,128]{3,2,1,0:T(2,128)(2,1)S(1)}, u32[]{:S(2)}, u32[]{:S(2)}) collective-permute-start(bf16[2,20,2,128]{3,2,1,0:T(2,128)(2,1)S(1)} %get-tuple-element.38), channel_id=1, source_target_pairs={{0,744},{1,745},{2,746},{3,747},{4,748},{5,749},{6,750},{7,751},{8... | collective-permute-start | bytes 61448 | tf_op jit(solution)/shard_map/ppermute | solution.py:25
  34.2 11.8 %collective-permute-start.4 = (f32[1152,128]{1,0:T(8,128)S(1)}, f32[1152,128]{1,0:T(8,128)S(1)}, u32[]{:S(2)}, u32[]{:S(2)}) collective-permute-start(f32[1152,128]{1,0:T(8,128)S(1)} %get-tuple-element.26), channel_id=1, source_target_pairs={{0,1},{1,0},{2,3},{3,2},{4,5},{5,4},{6,7},{7,6},{8,9},{9,8},{10,11... | collective-permute-start | bytes 1769480 | tf_op jit(solution)/shard_map/ppermute | solution.py:228
  94.2 8.4 %collective-permute-start.5 = (bf16[1152,128]{1,0:T(8,128)(2,1)S(1)}, bf16[1152,128]{1,0:T(8,128)(2,1)S(1)}, u32[]{:S(2)}, u32[]{:S(2)}) collective-permute-start(bf16[1152,128]{1,0:T(8,128)(2,1)S(1)} %bitcast.28), channel_id=1, source_target_pairs={{0,1},{1,0},{2,3},{3,2},{4,5},{5,4},{6,7},{7,6},{8,9},{9,8},{10,11... | collective-permute-start | bytes 884744 | tf_op jit(solution)/shard_map/ppermute | solution.py:228
